TPU v7x, 256 devices: a whole 4x4x8 slice. The times are simulated.
256 devices in a mesh: path: 32 (over x, z), mp: 8 (over y, core).
Axes of the slice: x: 4, y: 4, z: 8, core: 2. Of those that a mesh axis runs over, the one named last changes fastest.
Arguments:
- tokens: bfloat16 [12288, 2048], P('path', 'mp'), may hold values from -6 to 6
- cotangent: bfloat16 [12288, 2048], P('path', 'mp'), may hold values from -6 to 6
- path_weights: bfloat16 [32, 3, 4096, 2048], P('path', None, 'mp'), may hold values from -6 to 6
- outer_weights: float32 [32, 3, 8, 8, 16, 2048], P('path', None, None, 'mp'), may hold values from -6 to 6
- momentum: bfloat16 [32, 3, 8, 8, 16, 2048], P('path', None, None, 'mp'), may hold values from -6 to 6
- assignment: int32 [3, 32], replicated, may hold values from 0 to 7, as said below
- owners: int32 [3, 8, 32], replicated, may hold values from 0 to 31, each once within a row
Outputs:
- outputs: bfloat16 [12288, 2048], P('path', 'mp')
- refreshed: bfloat16 [32, 3, 8, 8, 16, 2048], P('path', None, None, 'mp')
Inputs may be any that keep to these rules, and one draw needn't show every extreme that they name: `assignment`: every one of the 8 modules of a level is used by at least one path; how many paths share a module varies from module to module. For each level and module, the owners of its 32 pieces are the 32 path indices, each once.
All inputs are finite; a program needn't handle non-finite values.
Results may differ from a plain program's by a relative error of at most 0.0068.
Values may be sent and summed in bfloat16 or wider, within the bound.
A program may use at most 128 MiB of HBM per device.

v0:
```python
import jax
import jax.numpy as jnp
from jax import lax
from jax.sharding import PartitionSpec as P

D = 2048
FF = 4096


mu_outer = 0.9
eta_outer = 0.7
lr_inner = 2.0


def contract(left, right, left_dim, right_dim):
    return lax.dot_general(
        left, right, (((left_dim,), (right_dim,)), ((), ())), preferred_element_type=jnp.float32
    )


def shards(tokens, cotangent, path_weights, outer_weights, momentum, assignment, owners):
    inputs, upstream = (
        lax.all_gather(tokens, "mp", axis=1, tiled=True),
        lax.all_gather(cotangent, "mp", axis=1, tiled=True),
    )
    weights = path_weights[0]
    levels = weights.shape[0]
    width = weights.shape[2]
    paths = lax.axis_size("path")
    modules = outer_weights.shape[2]
    block = outer_weights.shape[4]
    scale_d = D ** (-0.5)
    scale_f = FF ** (-0.5)
    level_ids = jnp.arange(levels, dtype=jnp.int32)
    mine = lax.dynamic_index_in_dim(assignment, lax.axis_index("path"), 1, keepdims=False)
    owner_rows = owners[level_ids, mine]
    path_ids = jnp.arange(paths, dtype=jnp.int32)
    inverse = jnp.sum(
        path_ids[None, :, None]
        * (owner_rows[:, :, None] == path_ids[None, None, :]).astype(jnp.int32),
        axis=1,
    )
    table = (assignment[:, None, :] == jnp.arange(modules, dtype=jnp.int32)[None, :, None]).astype(
        jnp.float32
    )
    shares = jnp.sum(table, axis=2)
    stored = outer_weights[0, :, :, 0]
    velocity_old = momentum[0, :, :, 0].astype(jnp.float32)
    gate = contract(inputs, weights[0], 1, 1) * scale_d
    upper = contract(inputs, weights[1], 1, 1) * scale_d
    sig = jax.nn.sigmoid(gate)
    act = gate * sig
    hidden = (act * upper).astype(jnp.bfloat16)
    grad_hidden = contract(upstream, weights[2], 1, 1) * scale_f
    pre_gate = (grad_hidden * upper * sig * (1.0 + gate * (1.0 - sig))).astype(jnp.bfloat16)
    pre_up = (grad_hidden * act).astype(jnp.bfloat16)

    def final_level(level):
        if level == 2:
            grad = contract(hidden, upstream, 0, 0) * scale_f
        elif level == 0:
            grad = contract(pre_gate, inputs, 0, 0) * scale_d
        else:
            grad = contract(pre_up, inputs, 0, 0) * scale_d
        return weights[level].astype(jnp.float32) - lr_inner * grad

    finals = jnp.stack([final_level(0), final_level(1), final_level(2)])
    count = finals.shape[0]
    blocks = finals.reshape(count, paths, block, width)
    received = lax.all_to_all(
        blocks[jnp.arange(count)[:, None], inverse], "path", split_axis=1, concat_axis=1, tiled=True
    )
    count = received.shape[0]
    sums = jnp.einsum("lmp,lpbd->lmbd", table, received, precision=lax.Precision.HIGHEST)
    mean = sums / shares[0 : 0 + count, :, None, None]
    delta = stored - mean
    velocity = mu_outer * velocity_old + delta
    fresh = (stored - eta_outer * (delta + mu_outer * velocity)).astype(jnp.bfloat16)
    fresh, leaving = (fresh, fresh[jnp.arange(count)[:, None], assignment])
    returned = lax.all_to_all(leaving, "path", split_axis=1, concat_axis=1, tiled=True)
    count = returned.shape[0]
    placed = returned[jnp.arange(count)[:, None], owner_rows]
    new_weights = placed.reshape(count, paths * block, width)
    gate_new = contract(inputs, new_weights[0], 1, 1) * scale_d
    upper_new = contract(inputs, new_weights[1], 1, 1) * scale_d
    hidden_new = (gate_new * jax.nn.sigmoid(gate_new) * upper_new).astype(jnp.bfloat16)
    partial_out = contract(hidden_new, new_weights[2], 1, 0) * scale_f
    outputs = lax.psum_scatter(partial_out, "mp", scatter_dimension=1, tiled=True).astype(
        jnp.bfloat16
    )
    refreshed = fresh.reshape(1, levels, modules, 1, block, width)
    return (outputs, refreshed)


def solution(mesh):
    return jax.shard_map(
        shards,
        mesh=mesh,
        in_specs=(
            P("path", "mp"),
            P("path", "mp"),
            P("path", None, "mp", None),
            P("path", None, None, "mp", None, None),
            P("path", None, None, "mp", None, None),
            P(),
            P(),
        ),
        out_specs=(P("path", "mp"), P("path", None, None, "mp", None, None)),
        check_vma=False,
    )
```

profile of v0, /device:TPU:1, one launch (start us, length us, event | category | flops | bytes accessed | tf_op | source)
XLA Modules:
  0.0 686.1 jit_solution(1793874220022884660)
XLA Ops:
  10.3 31.2 %all-gather.5.cloned.1.call-done = bf16[384,2048]{1,0:T(8,128)(2,1)} async-done(((bf16[384,256]{1,0:T(8,128)(2,1)}), bf16[384,2048]{1,0:T(8,128)(2,1)}) %all-gather.5.cloned.1.call-update) | async-done | bytes 1572880 | tf_op jit(solution)/shard_map/all_gather | solution.py:23
  41.5 4.1 fusion.18
  45.6 3.5 fusion.24
  49.1 22.7 %all-gather.3.cloned.1.call-done = bf16[384,2048]{1,0:T(8,128)(2,1)} async-done(((bf16[384,256]{1,0:T(8,128)(2,1)}), bf16[384,2048]{1,0:T(8,128)(2,1)}) %all-gather.3.cloned.1.call-update) | async-done | bytes 1572880 | tf_op jit(solution)/shard_map/all_gather | solution.py:24
  71.8 3.2 fusion.21
  75.1 3.1 multiply_subtract_fusion.1
  78.3 3.4 multiply_subtract_fusion.2
  81.7 3.3 multiply_subtract_fusion
  85.0 10.0 %pad_maximum_fusion = f32[3,32,16,2048]{3,2,1,0:T(8,128)} fusion(f32[1,32,16,2048]{3,2,1,0:T(8,128)} %bitcast.89, f32[1,32,16,2048]{3,2,1,0:T(8,128)S(1)} %bitcast.87, f32[1,32,16,2048]{3,2,1,0:T(8,128)} %bitcast.88), kind=kLoop, calls=%fused_computation.4 | loop fusion | flops 6291456 | bytes 25165824 | tf_op jit(solution)/shard_map/stack | solution.py:67
  95.0 13.8 %gather_fusion.1 = f32[96,16,2048]{2,1,0:T(8,128)} fusion(f32[3,32,16,2048]{3,2,1,0:T(8,128)} %pad_maximum_fusion, s32[96]{0:T(128)S(1)} %reshape.68), kind=kCustom, calls=%fused_computation.1 | custom fusion | bytes 25166592 | tf_op jit(solution)/shard_map/gather | solution.py:71
  108.8 11.3 %copy.30 = f32[3,32,16,2048]{3,2,0,1:T(8,128)} copy(f32[3,32,16,2048]{3,2,1,0:T(8,128)} %bitcast.84) | data formatting | bytes 25165824 | tf_op jit(solution)/shard_map/gather | solution.py:71
  120.1 10.0 %all-to-all-start = ((f32[3,32,16,2048]{3,2,0,1:T(8,128)}), f32[3,32,16,2048]{3,2,0,1:T(8,128)}, u32[]{:S(2)}, u32[]{:S(2)}) async-start(f32[3,32,16,2048]{3,2,0,1:T(8,128)} %copy.30), calls=%async_computation | async-start | bytes 25165824 | tf_op jit(solution)/shard_map/all_to_all | solution.py:70
  130.2 287.7 %all-to-all-done = f32[3,32,16,2048]{3,2,0,1:T(8,128)} async-done(((f32[3,32,16,2048]{3,2,0,1:T(8,128)}), f32[3,32,16,2048]{3,2,0,1:T(8,128)}, u32[]{:S(2)}, u32[]{:S(2)}) %all-to-all-start) | async-done | bytes 12582944 | tf_op jit(solution)/shard_map/all_to_all | solution.py:70
  417.9 18.8 %fusion.6 = bf16[3,8,16,2048]{3,1,2,0:T(8,128)(2,1)S(1)} fusion(f32[1,3,8,1,16,2048]{5,4,3,2,1,0:T(8,128)} %param.10, f32[3,32,16,2048]{3,2,0,1:T(8,128)} %all-to-all-done, bf16[1,3,8,1,16,2048]{5,4,3,2,1,0:T(8,128)(2,1)S(1)} %copy-done.3, f32[3,8]{1,0:T(4,128)S(1)} %convert_reduce_fusion, s32[3,32]{1,0:T(4,128)S(1)} %copy-done.2), kind=kOutput, calls=%fused_computation.15 | convolution fusion | flops 309854976 | bytes 18874848 | tf_op jit(solution)/shard_map/lmp,lpbd->lmbd/dot_general | solution.py:74
  437.7 6.6 gather_fusion.2
  444.3 6.6 copy.34
  450.8 21.9 %all-to-all-start.1 = ((bf16[3,32,16,2048]{3,2,0,1:T(8,128)(2,1)}), bf16[3,32,16,2048]{3,2,0,1:T(8,128)(2,1)}, u32[]{:S(2)}, u32[]{:S(2)}) async-start(bf16[3,32,16,2048]{3,2,0,1:T(8,128)(2,1)} %copy.34), calls=%async_computation.1 | async-start | bytes 12582912 | tf_op jit(solution)/shard_map/all_to_all | solution.py:80
  472.9 139.0 %all-to-all-done.1 = bf16[3,32,16,2048]{3,2,0,1:T(8,128)(2,1)} async-done(((bf16[3,32,16,2048]{3,2,0,1:T(8,128)(2,1)}), bf16[3,32,16,2048]{3,2,0,1:T(8,128)(2,1)}, u32[]{:S(2)}, u32[]{:S(2)}) %all-to-all-start.1) | async-done | bytes 6291488 | tf_op jit(solution)/shard_map/all_to_all | solution.py:80
  611.9 6.6 copy.35
  618.4 9.4 %gather_fusion.3 = bf16[96,16,2048]{2,1,0:T(8,128)(2,1)} fusion(bf16[3,32,16,2048]{3,2,1,0:T(8,128)(2,1)} %copy.35, s32[96]{0:T(128)S(1)} %reshape.80), kind=kCustom, calls=%fused_computation.3 | custom fusion | bytes 12583680 | tf_op jit(solution)/shard_map/gather | solution.py:82
  627.8 6.1 fusion.64
  635.8 6.1 convolution_multiply_fusion
  642.0 2.0 copy.38
  644.0 33.9 %reduce-scatter.2.cloned.1.call-done = f32[384,256]{1,0:T(8,128)} async-done(((f32[384,2048]{1,0:T(8,128)}), f32[384,256]{1,0:T(8,128)}) %reduce-scatter.2.cloned.1.call-update) | async-done | bytes 393232 | tf_op jit(solution)/shard_map/reduce_scatter | solution.py:88
  (42 shorter events, 7.9 us)
Async XLA Ops:
  7.2 2.4 copy-start
  7.2 34.3 %all-gather.5.cloned.1.call-start = ((), (), s32[]{:S(2)}) async-start(), calls=%async_computation.4 | async-start | bytes 1769472 | tf_op jit(solution)/shard_map/all_gather | solution.py:23
  7.9 63.9 %all-gather.3.cloned.1.call-start = ((), (), s32[]{:S(2)}) async-start(), calls=%async_computation.3 | async-start | bytes 1769472 | tf_op jit(solution)/shard_map/all_gather | solution.py:24
  41.5 4.1 copy-start.4
  71.8 3.2 copy-start.7
  71.8 6.4 slice-start
  75.1 3.1 slice-start.1
  75.1 3.1 copy-start.8
  78.2 3.4 copy-start.6
  120.1 10.0 %copy-start.2 = (s32[3,32]{1,0:T(4,128)S(1)}, s32[3,32]{1,0:T(4,128)}, u32[]{:S(2)}) copy-start(s32[3,32]{1,0:T(4,128)} %param.12) | copy-start | bytes 1156
  120.1 297.9 %copy-start.3 = (bf16[1,3,8,1,16,2048]{5,4,3,2,1,0:T(8,128)(2,1)S(1)}, bf16[1,3,8,1,16,2048]{5,4,3,2,1,0:T(8,128)(2,1)}, u32[]{:S(2)}) copy-start(bf16[1,3,8,1,16,2048]{5,4,3,2,1,0:T(8,128)(2,1)} %param.11) | copy-start | bytes 4718596
  120.1 297.8 %all-to-all-start = ((f32[3,32,16,2048]{3,2,0,1:T(8,128)}), f32[3,32,16,2048]{3,2,0,1:T(8,128)}, u32[]{:S(2)}, u32[]{:S(2)}) async-start(f32[3,32,16,2048]{3,2,0,1:T(8,128)} %copy.30), calls=%async_computation | async-start | bytes 25165824 | tf_op jit(solution)/shard_map/all_to_all | solution.py:70
  450.8 161.0 %all-to-all-start.1 = ((bf16[3,32,16,2048]{3,2,0,1:T(8,128)(2,1)}), bf16[3,32,16,2048]{3,2,0,1:T(8,128)(2,1)}, u32[]{:S(2)}, u32[]{:S(2)}) async-start(bf16[3,32,16,2048]{3,2,0,1:T(8,128)(2,1)} %copy.34), calls=%async_computation.1 | async-start | bytes 12582912 | tf_op jit(solution)/shard_map/all_to_all | solution.py:80
  472.7 205.1 %reduce-scatter.2.cloned.1.call-start = ((), (), s32[]{:S(2)}) async-start(), calls=%async_computation.5 | async-start | bytes 3538944 | tf_op jit(solution)/shard_map/reduce_scatter | solution.py:88
  627.8 6.1 copy-start.5
  641.9 37.6 %copy-start.1 = (s32[3,8,32]{2,1,0:T(8,128)S(1)}, s32[3,8,32]{2,1,0:T(8,128)}, u32[]{:S(2)}) copy-start(s32[3,8,32]{2,1,0:T(8,128)} %param.13) | copy-start | bytes 9220
Sparse Core Ops, SparseCore 0:
  9.8 31.6 all-gather.4
  43.3 28.4 all-gather.2
  642.1 35.7 reduce-scatter.1
where the time goes:
time: 688 us; the launch traced here: 686 us
  waiting for transfers between devices  516 us (75%)
  local copies, waits for them, and re-layouts  64.1 us (9%)
  matrix products  47.5 us (7%)
  starting transfers between devices  32 us (5%)
  between operations  13.9 us (2%)
  other arithmetic  12.8 us (2%)
    all_to_all x1, waiting for transfers between devices, shards(): lax.all_to_all(blocks[jnp.arange(count)[:, None], inverse], 'path', split...  288 us
    all_to_all x1, waiting for transfers between devices, shards(): lax.all_to_all(leaving, 'path', split_axis=1, concat_axis=1, tiled=True)  139 us
    reduce_scatter x1, waiting for transfers between devices, shards(): lax.psum_scatter(partial_out, 'mp', scatter_dimension=1, tiled=True)  33.9 us
    all_gather x1, waiting for transfers between devices, shards(): lax.all_gather(tokens, 'mp', axis=1, tiled=True)  31.2 us
    dot_general x8, matrix products, contract(): lax.dot_general(left, right, (((left_dim,), (right_dim,)), ((), ())), pre...  28.6 us
    gather x2, local copies, waits for them, and re-layouts, shards(): blocks[jnp.arange(count)[:, None], inverse]  25.1 us
    all_gather x1, waiting for transfers between devices, shards(): lax.all_gather(cotangent, 'mp', axis=1, tiled=True)  22.7 us
    all_to_all x1, starting transfers between devices, shards(): lax.all_to_all(leaving, 'path', split_axis=1, concat_axis=1, tiled=True)  21.9 us
  transfers between devices with their start and end apart: 5, of which 5 were waited for; matrix products, arithmetic and copies ran while one was open for 2% of the time, Pallas kernels for 0%

commit v1 on v0

--- a/solution.py
+++ b/solution.py
@@ -62,7 +62,7 @@
             grad = contract(pre_gate, inputs, 0, 0) * scale_d
         else:
             grad = contract(pre_up, inputs, 0, 0) * scale_d
-        return weights[level].astype(jnp.float32) - lr_inner * grad
+        return (weights[level].astype(jnp.float32) - lr_inner * grad).astype(jnp.bfloat16)
 
     finals = jnp.stack([final_level(0), final_level(1), final_level(2)])
     count = finals.shape[0]
@@ -71,7 +71,9 @@
         blocks[jnp.arange(count)[:, None], inverse], "path", split_axis=1, concat_axis=1, tiled=True
     )
     count = received.shape[0]
-    sums = jnp.einsum("lmp,lpbd->lmbd", table, received, precision=lax.Precision.HIGHEST)
+    sums = jnp.einsum(
+        "lmp,lpbd->lmbd", table.astype(jnp.bfloat16), received, preferred_element_type=jnp.float32
+    )
     mean = sums / shares[0 : 0 + count, :, None, None]
     delta = stored - mean
     velocity = mu_outer * velocity_old + delta
@@ -85,9 +87,11 @@
     upper_new = contract(inputs, new_weights[1], 1, 1) * scale_d
     hidden_new = (gate_new * jax.nn.sigmoid(gate_new) * upper_new).astype(jnp.bfloat16)
     partial_out = contract(hidden_new, new_weights[2], 1, 0) * scale_f
-    outputs = lax.psum_scatter(partial_out, "mp", scatter_dimension=1, tiled=True).astype(
-        jnp.bfloat16
-    )
+    mp = lax.axis_size("mp")
+    rows = partial_out.shape[0]
+    slices = partial_out.astype(jnp.bfloat16).reshape(rows, mp, -1).swapaxes(0, 1)
+    arrived = lax.all_to_all(slices, "mp", split_axis=0, concat_axis=0, tiled=True)
+    outputs = jnp.sum(arrived.astype(jnp.float32), axis=0).astype(jnp.bfloat16)
     refreshed = fresh.reshape(1, levels, modules, 1, block, width)
     return (outputs, refreshed)
 

time: 688 us -> 492 us (0.72)
  waiting for transfers between devices: 516 us -> 355 us
  matrix products: 47.5 us -> 37.9 us
  starting transfers between devices: 32 us -> 23.7 us
  local copies, waits for them, and re-layouts: 64.1 us -> 56.5 us
  other arithmetic: 12.8 us -> 5.26 us
    all_to_all x1, waiting for transfers between devices: 288 us -> 140 us  [shards(): lax.all_to_all(blocks[jnp.arange(count)[:, None], inverse], 'path', split...]
    reduce_scatter x1 -> x0, waiting for transfers between devices: 33.9 us -> none  [shards(): lax.psum_scatter(partial_out, 'mp', scatter_dimension=1, tiled=True)]
    all_to_all x0 -> x1, waiting for transfers between devices: none -> 18.6 us  [shards(): lax.all_to_all(slices, 'mp', split_axis=0, concat_axis=0, tiled=True)]
    all_to_all x1, starting transfers between devices: 21.9 us -> 8.29 us  [shards(): lax.all_to_all(leaving, 'path', split_axis=1, concat_axis=1, tiled=True)]
    gather x2, local copies, waits for them, and re-layouts: 25.1 us -> 16 us  [shards(): blocks[jnp.arange(count)[:, None], inverse]]
where the time goes in v1:
time: 492 us
  waiting for transfers between devices  355 us (72%)
  local copies, waits for them, and re-layouts  56.5 us (11%)
  matrix products  37.9 us (8%)
  starting transfers between devices  23.7 us (5%)
  between operations  14.2 us (3%)
  other arithmetic  5.26 us (1%)
    all_to_all x1, waiting for transfers between devices, shards(): lax.all_to_all(blocks[jnp.arange(count)[:, None], inverse], 'path', split...  140 us
    all_to_all x1, waiting for transfers between devices, shards(): lax.all_to_all(leaving, 'path', split_axis=1, concat_axis=1, tiled=True)  140 us
    all_gather x1, waiting for transfers between devices, shards(): lax.all_gather(tokens, 'mp', axis=1, tiled=True)  31.2 us
    dot_general x8, matrix products, contract(): lax.dot_general(left, right, (((left_dim,), (right_dim,)), ((), ())), pre...  23.6 us
    all_gather x1, waiting for transfers between devices, shards(): lax.all_gather(cotangent, 'mp', axis=1, tiled=True)  22.7 us
    all_to_all x1, waiting for transfers between devices, shards(): lax.all_to_all(slices, 'mp', split_axis=0, concat_axis=0, tiled=True)  18.6 us
    gather x2, local copies, waits for them, and re-layouts, shards(): blocks[jnp.arange(count)[:, None], inverse]  16 us
    dot_general x1, matrix products, shards(): jnp.einsum('lmp,lpbd->lmbd', table.astype(jnp.bfloat16), received, prefer...  14.2 us
  transfers between devices with their start and end apart: 5, of which 5 were waited for; matrix products, arithmetic and copies ran while one was open for 2% of the time, Pallas kernels for 0%

profile of v1, /device:TPU:1, one launch (start us, length us, event | category | flops | bytes accessed | tf_op | source)
XLA Modules:
  0.0 492.1 jit_solution(2362759124659216805)
XLA Ops:
  10.3 31.2 %all-gather.5.cloned.1.call-done = bf16[384,2048]{1,0:T(8,128)(2,1)} async-done(((bf16[384,256]{1,0:T(8,128)(2,1)}), bf16[384,2048]{1,0:T(8,128)(2,1)}) %all-gather.5.cloned.1.call-update) | async-done | bytes 1572880 | tf_op jit(solution)/shard_map/all_gather | solution.py:23
  41.5 4.1 fusion.18
  45.6 3.5 fusion.24
  49.1 22.7 %all-gather.3.cloned.1.call-done = bf16[384,2048]{1,0:T(8,128)(2,1)} async-done(((bf16[384,256]{1,0:T(8,128)(2,1)}), bf16[384,2048]{1,0:T(8,128)(2,1)}) %all-gather.3.cloned.1.call-update) | async-done | bytes 1572880 | tf_op jit(solution)/shard_map/all_gather | solution.py:24
  71.8 3.2 fusion.21
  75.1 3.1 subtract_convert_fusion
  81.2 3.3 pad_maximum_fusion
  84.5 9.4 %gather_fusion.1 = bf16[96,16,2048]{2,1,0:T(8,128)(2,1)} fusion(bf16[3,32,16,2048]{3,2,1,0:T(8,128)(2,1)} %pad_maximum_fusion, s32[96]{0:T(128)S(1)} %reshape.72), kind=kCustom, calls=%fused_computation.1 | custom fusion | bytes 12583680 | tf_op jit(solution)/shard_map/gather | solution.py:71
  93.9 6.6 %copy.31 = bf16[3,32,16,2048]{3,2,0,1:T(8,128)(2,1)} copy(bf16[3,32,16,2048]{3,2,1,0:T(8,128)(2,1)} %bitcast.91) | data formatting | bytes 12582912 | tf_op jit(solution)/shard_map/gather | solution.py:71
  100.5 10.0 %all-to-all-start = ((bf16[3,32,16,2048]{3,2,0,1:T(8,128)(2,1)}), bf16[3,32,16,2048]{3,2,0,1:T(8,128)(2,1)}, u32[]{:S(2)}, u32[]{:S(2)}) async-start(bf16[3,32,16,2048]{3,2,0,1:T(8,128)(2,1)} %copy.31), calls=%async_computation | async-start | bytes 12582912 | tf_op jit(solution)/shard_map/all_to_all | solution.py:70
  110.6 140.5 %all-to-all-done = bf16[3,32,16,2048]{3,2,0,1:T(8,128)(2,1)} async-done(((bf16[3,32,16,2048]{3,2,0,1:T(8,128)(2,1)}), bf16[3,32,16,2048]{3,2,0,1:T(8,128)(2,1)}, u32[]{:S(2)}, u32[]{:S(2)}) %all-to-all-start) | async-done | bytes 6291488 | tf_op jit(solution)/shard_map/all_to_all | solution.py:70
  251.1 14.2 %fusion.6 = bf16[3,8,16,2048]{3,1,2,0:T(8,128)(2,1)S(1)} fusion(f32[1,3,8,1,16,2048]{5,4,3,2,1,0:T(8,128)} %param.10, bf16[3,32,16,2048]{3,2,0,1:T(8,128)(2,1)} %all-to-all-done, bf16[1,3,8,1,16,2048]{5,4,3,2,1,0:T(8,128)(2,1)S(1)} %copy-done.3, f32[3,8]{1,0:T(4,128)S(1)} %convert_reduce_fusion, s32[3,32]{1,0:T(4,128)S(1)} %copy-done.2), kind=kOutput, calls=%fused_computation.15 | convolution fusion | flops 58198272 | bytes 12583392 | tf_op jit(solution)/shard_map/lmp,lpbd->lmbd/dot_general | solution.py:74
  266.2 6.8 %gather_fusion.2 = bf16[96,16,2048]{2,1,0:T(8,128)(2,1)} fusion(bf16[3,8,16,2048]{3,2,1,0:T(8,128)(2,1)S(1)} %copy.34, s32[96]{0:T(128)S(1)} %reshape.78), kind=kCustom, calls=%fused_computation.2 | custom fusion | bytes 12583680 | tf_op jit(solution)/shard_map/gather | solution.py:81
  273.0 6.6 %copy.35 = bf16[3,32,16,2048]{3,2,0,1:T(8,128)(2,1)} copy(bf16[3,32,16,2048]{3,2,1,0:T(8,128)(2,1)} %bitcast.92) | data formatting | bytes 12582912 | tf_op jit(solution)/shard_map/gather | solution.py:81
  279.6 8.3 %all-to-all-start.1 = ((bf16[3,32,16,2048]{3,2,0,1:T(8,128)(2,1)}), bf16[3,32,16,2048]{3,2,0,1:T(8,128)(2,1)}, u32[]{:S(2)}, u32[]{:S(2)}) async-start(bf16[3,32,16,2048]{3,2,0,1:T(8,128)(2,1)} %copy.35), calls=%async_computation.1 | async-start | bytes 12582912 | tf_op jit(solution)/shard_map/all_to_all | solution.py:82
  288.0 140.3 %all-to-all-done.1 = bf16[3,32,16,2048]{3,2,0,1:T(8,128)(2,1)} async-done(((bf16[3,32,16,2048]{3,2,0,1:T(8,128)(2,1)}), bf16[3,32,16,2048]{3,2,0,1:T(8,128)(2,1)}, u32[]{:S(2)}, u32[]{:S(2)}) %all-to-all-start.1) | async-done | bytes 6291488 | tf_op jit(solution)/shard_map/all_to_all | solution.py:82
  428.3 6.6 %copy.36 = bf16[3,32,16,2048]{3,2,1,0:T(8,128)(2,1)} copy(bf16[3,32,16,2048]{3,2,0,1:T(8,128)(2,1)} %all-to-all-done.1) | data formatting | bytes 12582912 | tf_op jit(solution)/shard_map/all_to_all | solution.py:82
  434.8 9.4 %gather_fusion.3 = bf16[96,16,2048]{2,1,0:T(8,128)(2,1)} fusion(bf16[3,32,16,2048]{3,2,1,0:T(8,128)(2,1)} %copy.36, s32[96]{0:T(128)S(1)} %reshape.84), kind=kCustom, calls=%fused_computation.3 | custom fusion | bytes 12583680 | tf_op jit(solution)/shard_map/gather | solution.py:84
  444.2 6.1 %fusion.64 = (bf16[32,16,2048]{2,1,0:T(8,128)(2,1)S(1)}, bf16[32,16,2048]{2,1,0:T(8,128)(2,1)}, bf16[32,16,2048]{2,1,0:T(8,128)(2,1)}) fusion(bf16[96,16,2048]{2,1,0:T(8,128)(2,1)} %gather_fusion.3), kind=kLoop, calls=%fused_computation.81 | loop fusion | bytes 12582912 | tf_op jit(solution)/shard_map/slice | solution.py:86
  450.4 1.9 fusion.28
  452.3 4.9 multiply_convert_fusion
  458.4 5.3 %all-to-all-start.2 = ((bf16[8,384,256]{2,1,0:T(8,128)(2,1)}), bf16[8,384,256]{2,1,0:T(8,128)(2,1)S(1)}, u32[]{:S(2)}, u32[]{:S(2)}) async-start(bf16[8,384,256]{2,1,0:T(8,128)(2,1)} %bitcast.94), calls=%async_computation.2 | async-start | bytes 3145728 | tf_op jit(solution)/shard_map/all_to_all | solution.py:93
  463.8 2.0 copy.40
  465.8 18.6 %all-to-all-done.2 = bf16[8,384,256]{2,1,0:T(8,128)(2,1)S(1)} async-done(((bf16[8,384,256]{2,1,0:T(8,128)(2,1)}), bf16[8,384,256]{2,1,0:T(8,128)(2,1)S(1)}, u32[]{:S(2)}, u32[]{:S(2)}) %all-to-all-start.2) | async-done | bytes 1572896 | tf_op jit(solution)/shard_map/all_to_all | solution.py:93
  (42 shorter events, 9.4 us)
Async XLA Ops:
  7.2 2.4 copy-start
  7.2 34.3 %all-gather.5.cloned.1.call-start = ((), (), s32[]{:S(2)}) async-start(), calls=%async_computation.4 | async-start | bytes 1769472 | tf_op jit(solution)/shard_map/all_gather | solution.py:23
  7.9 63.9 %all-gather.3.cloned.1.call-start = ((), (), s32[]{:S(2)}) async-start(), calls=%async_computation.3 | async-start | bytes 1769472 | tf_op jit(solution)/shard_map/all_gather | solution.py:24
  41.5 4.1 copy-start.4
  71.8 3.2 copy-start.6
  71.8 3.3 copy-start.7
  71.8 3.3 copy-start.8
  71.8 6.4 %slice-start = ((s8[6291456]{0:T(1024)(128)(4,1)}), s8[4194304]{0:T(1024)(128)(4,1)S(1)}, s32[]{:S(2)}) async-start(s8[6291456]{0:T(1024)(128)(4,1)} %bitcast.102), calls=%async_computation.5 | async-start | bytes 8388608
  75.1 3.2 slice-start.1
  100.4 10.0 %copy-start.2 = (s32[3,32]{1,0:T(4,128)S(1)}, s32[3,32]{1,0:T(4,128)}, u32[]{:S(2)}) copy-start(s32[3,32]{1,0:T(4,128)} %param.12) | copy-start | bytes 1156
  100.4 150.6 %copy-start.3 = (bf16[1,3,8,1,16,2048]{5,4,3,2,1,0:T(8,128)(2,1)S(1)}, bf16[1,3,8,1,16,2048]{5,4,3,2,1,0:T(8,128)(2,1)}, u32[]{:S(2)}) copy-start(bf16[1,3,8,1,16,2048]{5,4,3,2,1,0:T(8,128)(2,1)} %param.11) | copy-start | bytes 4718596
  100.5 150.6 %all-to-all-start = ((bf16[3,32,16,2048]{3,2,0,1:T(8,128)(2,1)}), bf16[3,32,16,2048]{3,2,0,1:T(8,128)(2,1)}, u32[]{:S(2)}, u32[]{:S(2)}) async-start(bf16[3,32,16,2048]{3,2,0,1:T(8,128)(2,1)} %copy.31), calls=%async_computation | async-start | bytes 12582912 | tf_op jit(solution)/shard_map/all_to_all | solution.py:70
  279.6 148.7 %all-to-all-start.1 = ((bf16[3,32,16,2048]{3,2,0,1:T(8,128)(2,1)}), bf16[3,32,16,2048]{3,2,0,1:T(8,128)(2,1)}, u32[]{:S(2)}, u32[]{:S(2)}) async-start(bf16[3,32,16,2048]{3,2,0,1:T(8,128)(2,1)} %copy.35), calls=%async_computation.1 | async-start | bytes 12582912 | tf_op jit(solution)/shard_map/all_to_all | solution.py:82
  444.2 6.1 %copy-start.5 = (bf16[384,2048]{1,0:T(8,128)(2,1)S(1)}, bf16[384,2048]{1,0:T(8,128)(2,1)}, u32[]{:S(2)}) copy-start(bf16[384,2048]{1,0:T(8,128)(2,1)} %all-gather.5.cloned.1.call-done) | copy-start | bytes 4718596
  458.4 25.9 %all-to-all-start.2 = ((bf16[8,384,256]{2,1,0:T(8,128)(2,1)}), bf16[8,384,256]{2,1,0:T(8,128)(2,1)S(1)}, u32[]{:S(2)}, u32[]{:S(2)}) async-start(bf16[8,384,256]{2,1,0:T(8,128)(2,1)} %bitcast.94), calls=%async_computation.2 | async-start | bytes 3145728 | tf_op jit(solution)/shard_map/all_to_all | solution.py:93
  463.8 21.5 %copy-start.1 = (s32[3,8,32]{2,1,0:T(8,128)S(1)}, s32[3,8,32]{2,1,0:T(8,128)}, u32[]{:S(2)}) copy-start(s32[3,8,32]{2,1,0:T(8,128)} %param.13) | copy-start | bytes 9220
Sparse Core Ops, SparseCore 0:
  9.8 31.6 all-gather.4
  43.3 28.4 all-gather.2

commit v2 on v1

--- a/solution.py
+++ b/solution.py
@@ -1,7 +1,11 @@
 import jax
 import jax.numpy as jnp
 from jax import lax
+from jax.experimental import pallas as pl
+from jax.experimental.pallas import tpu as pltpu
 from jax.sharding import PartitionSpec as P
+
+MESH = pl.DeviceIdType.MESH
 
 D = 2048
 FF = 4096
@@ -10,6 +14,293 @@
 mu_outer = 0.9
 eta_outer = 0.7
 lr_inner = 2.0
+
+NX = 4
+NZ = 8
+KORD = (4, 3, 5, 2, 6, 1, 7, 0)
+POS = {k: i for i, k in enumerate(KORD)}
+GROUPS = ((0, 1), (1, 3), (3, 5), (5, 7), (7, 8))
+M = 8
+LV = 3
+B = 16
+HALF = D // 2
+CH = 256
+SIGN = (-1, 1)
+
+
+def exchange_kernel(
+    mask, pick, rcp, finals, outer, momentum, returned, refreshed, *scratch
+):
+    it = iter(scratch)
+    take = lambda n: [next(it) for _ in range(n)]
+    pairs = lambda: [take(2) for _ in range(LV)]
+    X = take(LV)
+    B0, B1o, B1f, T2, B2, B3 = (pairs() for _ in range(6))
+    F = take(LV)
+    C1, C2, C3d, S2, C3s, S3, C4 = (pairs() for _ in range(7))
+    Y = take(LV)
+    O, V = take(LV), take(LV)
+    xs, xr, zs, zr, ls = take(5)
+    me = lax.axis_index("path")
+    x, z = me // NZ, lax.rem(me, NZ)
+    right = [lax.rem(x + dx, NX) * NZ + z for dx in range(NX)]
+    along = [x * NZ + lax.rem(z + NZ + s, NZ) for s in SIGN]
+
+    barrier = pltpu.get_barrier_semaphore()
+    for other in right[1:] + along:
+        pl.semaphore_signal(barrier, inc=1, device_id={"path": other}, device_id_type=MESH)
+    pl.semaphore_wait(barrier, 5)
+
+    started = []
+    zc = {}
+    xc = {}
+
+    def local(key, src, dst, index):
+        c = pltpu.make_async_copy(src, dst, ls.at[index])
+        c.start()
+        xc[key] = c
+
+    def remote(table, key, src, dst, ssem, rsem, other):
+        c = pltpu.make_async_remote_copy(
+            src_ref=src, dst_ref=dst, send_sem=ssem, recv_sem=rsem,
+            device_id={"path": other}, device_id_type=MESH,
+        )
+        c.start()
+        started.append(c)
+        table[key] = c
+
+    def zsend(l, s, step, src, dst):
+        remote(zc, (l, s, step), src, dst, zs.at[l, s, step], zr.at[l, s, step], along[s])
+
+    def zwait(l, s, step):
+        zc[l, s, step].wait_recv()
+
+    def xwait(l, g):
+        for dx in range(1, NX):
+            xc[l, g, dx].wait_recv()
+
+    def combine(dst, bases, terms, lo, hi):
+        def body(c, carry):
+            col = pl.multiple_of(lo + c * CH, CH)
+            vals = [
+                (ref[idx, :, pl.ds(pl.multiple_of(col - off, CH), CH)].astype(jnp.float32), at)
+                for ref, idx, off, at in terms
+            ]
+            for m in range(M):
+                acc = None
+                for base in bases:
+                    v = base[m, :, pl.ds(col, CH)].astype(jnp.float32)
+                    acc = v if acc is None else acc + v
+                for v, at in vals:
+                    t = v * mask[at + m]
+                    acc = t if acc is None else acc + t
+                dst(m, col, acc)
+            return carry
+
+        lax.fori_loop(0, (hi - lo) // CH, body, 0)
+
+    def at(l, j, r):
+        return ((l * NZ + j % NZ) * NX + r) * M
+
+    def own(l, k):
+        return [(X[l].at[POS[k % NZ]], r, 0, at(l, 0, r)) for r in range(NX)]
+
+    def into(ref):
+        def put(m, col, acc):
+            ref[m, :, pl.ds(col, CH)] = acc.astype(jnp.bfloat16)
+        return put
+
+    def a0(l):
+        if l == 0:
+            for i in range(LV):
+                local(("o", i), outer.at[i], O[i], 6 + i)
+                local(("v", i), momentum.at[i], V[i], 9 + i)
+        local((l, "own"), finals.at[l, 0], X[l].at[:, 0], l)
+        for g, (lo, hi) in enumerate(GROUPS):
+            for dx in (1, 3, 2):
+                remote(
+                    xc, (l, g, dx), finals.at[l, dx, pl.ds(lo, hi - lo)],
+                    X[l].at[pl.ds(lo, hi - lo), dx], xs.at[0, l, g, dx - 1], xr.at[0, l, g, dx - 1],
+                    right[dx],
+                )
+
+    def a1(l):
+        xc[l, "own"].wait()
+        xwait(l, 0)
+        for s in (0, 1):
+            zsend(l, s, 0, X[l].at[0, :, :, pl.ds(s * HALF, HALF)], B0[l][s])
+
+    def a2(l):
+        xwait(l, 1)
+        for s in (0, 1):
+            zsend(l, s, 1, X[l].at[POS[3 * SIGN[s] % NZ]], B1o[l][s])
+        for s in (0, 1):
+            zwait(l, s, 0)
+            zsend(l, s, 2, B0[l][s], B1f[l][s])
+
+    def a3(l):
+        xwait(l, 2)
+        for s in (0, 1):
+            sg = SIGN[s]
+            zwait(l, s, 1)
+            near = own(l, 2 * sg) + [(B1o[l][s], r, 0, at(l, -sg, r)) for r in range(NX)]
+            o = (1 - s) * HALF
+            combine(into(T2[l][s]), [], near, o, o + HALF)
+            zwait(l, s, 2)
+            o = s * HALF
+            far = [(B1f[l][s], r, o, at(l, -2 * sg, r)) for r in range(NX)]
+            combine(into(T2[l][s]), [], near + far, o, o + HALF)
+            zsend(l, s, 3, T2[l][s], B2[l][s])
+
+    def a4(l):
+        xwait(l, 3)
+        for s in (0, 1):
+            zwait(l, s, 3)
+            combine(into(B2[l][s]), [B2[l][s]], own(l, SIGN[s]), 0, D)
+            zsend(l, s, 4, B2[l][s], B3[l][s])
+
+    def stage(l, k, src):
+        i = POS[k % NZ]
+        for dx in range(NX):
+            src(i, dx, pick[(l * NZ) * NX + dx])
+
+    def xsend(l, g):
+        lo, hi = GROUPS[g]
+        n = hi - lo
+        for dx in (1, 3, 2):
+            remote(
+                xc, (l, g, dx, "r"), Y[l].at[dx, pl.ds(lo, n)], returned.at[l, dx, pl.ds(lo, n)],
+                xs.at[1, l, g, dx - 1], xr.at[1, l, g, dx - 1], right[dx],
+            )
+
+    def a5(l):
+        xwait(l, 4)
+        xc["o", l].wait()
+        xc["v", l].wait()
+        for s in (0, 1):
+            zwait(l, s, 4)
+
+        def put(m, col, acc):
+            cols = pl.ds(col, CH)
+            stored = O[l][m, :, cols]
+            delta = stored - acc * rcp[l * M + m]
+            velocity = mu_outer * V[l][m, :, cols].astype(jnp.float32) + delta
+            F[l][m, :, cols] = (stored - eta_outer * (delta + mu_outer * velocity)).astype(jnp.bfloat16)
+
+        combine(put, [B3[l][0], B3[l][1]], own(l, 0), 0, D)
+        for s in (0, 1):
+            zsend(l, s, 5, F[l], C1[l][s])
+        local((l, "fresh"), F[l], refreshed.at[l], 3 + l)
+
+        def src(i, dx, a):
+            Y[l][dx, i] = F[l][a]
+
+        stage(l, 0, src)
+        xsend(l, 4)
+
+    def a6(l):
+        for s in (0, 1):
+            zwait(l, s, 5)
+            zsend(l, s, 6, C1[l][s], C2[l][s])
+        for s in (0, 1):
+            def src(i, dx, a):
+                Y[l][dx, i] = C1[l][s][a]
+
+            stage(l, -SIGN[s], src)
+        xsend(l, 3)
+
+    def a7(l):
+        for s in (0, 1):
+            zwait(l, s, 6)
+            zsend(l, s, 7, C2[l][s].at[:, :, pl.ds(s * HALF, HALF)], C3d[l][s])
+            j = SIGN[s] % NZ
+            for dx in range(NX):
+                a = pick[(l * NZ + j) * NX + dx]
+                S2[l][s][dx] = C2[l][s][a, :, pl.ds((1 - s) * HALF, HALF)]
+            zsend(l, s, 8, S2[l][s], C3s[l][s])
+        for s in (0, 1):
+            def src(i, dx, a):
+                Y[l][dx, i] = C2[l][s][a]
+
+            stage(l, -2 * SIGN[s], src)
+        xsend(l, 2)
+
+    def a8(l):
+        for s in (0, 1):
+            zwait(l, s, 7)
+            j = SIGN[s] % NZ
+            for dx in range(NX):
+                a = pick[(l * NZ + j) * NX + dx]
+                S3[l][s][dx] = C3d[l][s][a]
+            zsend(l, s, 9, S3[l][s], C4[l][s])
+        for s in (0, 1):
+            zwait(l, s, 8)
+
+            def src(i, dx, a):
+                Y[l][dx, i, :, pl.ds(s * HALF, HALF)] = C3d[l][s][a]
+                Y[l][dx, i, :, pl.ds((1 - s) * HALF, HALF)] = C3s[l][s][dx]
+
+            stage(l, -3 * SIGN[s], src)
+        xsend(l, 1)
+
+    def a9(l):
+        for s in (0, 1):
+            zwait(l, s, 9)
+        def src(i, dx, a):
+            for s in (0, 1):
+                Y[l][dx, i, :, pl.ds(s * HALF, HALF)] = C4[l][s][dx]
+
+        stage(l, 4, src)
+        xsend(l, 0)
+        local((l, "mine"), Y[l].at[0], returned.at[l, 0], 12 + l)
+
+    def a10(l):
+        for g in range(len(GROUPS)):
+            for dx in range(1, NX):
+                xc[l, g, dx, "r"].wait_recv()
+        xc[l, "mine"].wait()
+        xc[l, "fresh"].wait()
+
+    steps = (a0, a1, a2, a3, a4, a5, a6, a7, a8, a9, a10)
+    for slot in range(len(steps) + (LV - 1)):
+        for l in range(LV):
+            if 0 <= slot - l < len(steps):
+                steps[slot - l](l)
+    for c in started:
+        c.wait_send()
+
+
+def exchange(mask, pick, rcp, finals, outer, momentum):
+    bf = lambda *shape: pltpu.VMEM(shape, jnp.bfloat16)
+    full, half = (D,), (HALF,)
+    dense, dense_half = bf(M, B, D), bf(M, B, HALF)
+    four, four_half = bf(NX, B, D), bf(NX, B, HALF)
+    pairs = lambda kind: [kind] * (2 * LV)
+    scratch = [bf(NZ, NX, B, D)] * LV
+    for kind in (four_half, four, four_half, dense, dense, dense):
+        scratch += pairs(kind)
+    scratch += [dense] * LV
+    for kind in (dense, dense, dense_half, four_half, four_half, four_half, four_half):
+        scratch += pairs(kind)
+    scratch += [bf(NX, NZ, B, D)] * LV
+    scratch += [pltpu.VMEM((M, B, D), jnp.float32)] * LV + [dense] * LV
+    dma = pltpu.SemaphoreType.DMA
+    scratch += [dma((2, LV, 5, 3)), dma((2, LV, 5, 3)), dma((LV, 2, 10)), dma((LV, 2, 10)), dma((15,))]
+    smem = pl.BlockSpec(memory_space=pltpu.SMEM)
+    anyw = pl.BlockSpec(memory_space=pl.ANY)
+    return pl.pallas_call(
+        exchange_kernel,
+        out_shape=(
+            jax.ShapeDtypeStruct((LV, NX, NZ, B, D), jnp.bfloat16),
+            jax.ShapeDtypeStruct((LV, M, B, D), jnp.bfloat16),
+        ),
+        in_specs=[smem, smem, smem, anyw, anyw, anyw],
+        out_specs=(anyw, anyw),
+        scratch_shapes=scratch,
+        compiler_params=pltpu.CompilerParams(
+            collective_id=0, has_side_effects=True, vmem_limit_bytes=62 * 1024 * 1024
+        ),
+    )(mask, pick, rcp, finals, outer, momentum)
 
 
 def contract(left, right, left_dim, right_dim):
@@ -40,12 +331,20 @@
         * (owner_rows[:, :, None] == path_ids[None, None, :]).astype(jnp.int32),
         axis=1,
     )
-    table = (assignment[:, None, :] == jnp.arange(modules, dtype=jnp.int32)[None, :, None]).astype(
-        jnp.float32
-    )
-    shares = jnp.sum(table, axis=2)
-    stored = outer_weights[0, :, :, 0]
-    velocity_old = momentum[0, :, :, 0].astype(jnp.float32)
+    here = lax.axis_index("path")
+    at_x, at_z = here // NZ, here % NZ
+    kord = jnp.array(KORD, dtype=jnp.int32)
+    xs, zs = jnp.arange(NX, dtype=jnp.int32), jnp.arange(NZ, dtype=jnp.int32)
+    ahead = ((at_x + xs) % NX)[:, None] * NZ + ((at_z + kord) % NZ)[None, :]
+    behind = ((at_x - xs) % NX)[:, None] * NZ + ((at_z + kord) % NZ)[None, :]
+    rows_z = (at_z + zs) % NZ
+    from_ids = ((at_x - xs) % NX)[None, :] * NZ + rows_z[:, None]
+    to_ids = ((at_x + xs) % NX)[None, :] * NZ + rows_z[:, None]
+    module_ids = jnp.arange(modules, dtype=jnp.int32)
+    mask = (assignment[:, from_ids][..., None] == module_ids).astype(jnp.float32).reshape(-1)
+    pick = assignment[:, to_ids].reshape(-1)
+    shares = jnp.sum((assignment[:, :, None] == module_ids).astype(jnp.float32), axis=1)
+    rcp = (1.0 / shares).reshape(-1)
     gate = contract(inputs, weights[0], 1, 1) * scale_d
     upper = contract(inputs, weights[1], 1, 1) * scale_d
     sig = jax.nn.sigmoid(gate)
@@ -67,21 +366,21 @@
     finals = jnp.stack([final_level(0), final_level(1), final_level(2)])
     count = finals.shape[0]
     blocks = finals.reshape(count, paths, block, width)
-    received = lax.all_to_all(
-        blocks[jnp.arange(count)[:, None], inverse], "path", split_axis=1, concat_axis=1, tiled=True
-    )
-    count = received.shape[0]
-    sums = jnp.einsum(
-        "lmp,lpbd->lmbd", table.astype(jnp.bfloat16), received, preferred_element_type=jnp.float32
-    )
-    mean = sums / shares[0 : 0 + count, :, None, None]
-    delta = stored - mean
-    velocity = mu_outer * velocity_old + delta
-    fresh = (stored - eta_outer * (delta + mu_outer * velocity)).astype(jnp.bfloat16)
-    fresh, leaving = (fresh, fresh[jnp.arange(count)[:, None], assignment])
-    returned = lax.all_to_all(leaving, "path", split_axis=1, concat_axis=1, tiled=True)
-    count = returned.shape[0]
-    placed = returned[jnp.arange(count)[:, None], owner_rows]
+    leaving = blocks[level_ids[:, None], inverse[:, ahead.reshape(-1)]]
+    returned, fresh = exchange(
+        mask,
+        pick,
+        rcp,
+        leaving.reshape(count, NX, NZ, block, width),
+        outer_weights.reshape(count, modules, block, width),
+        momentum.reshape(count, modules, block, width),
+    )
+    slot_of = jnp.sum(
+        jnp.where(behind.reshape(-1)[None, :] == path_ids[:, None], path_ids[None, :], 0), axis=1
+    )
+    placed = returned.reshape(count, paths, block, width)[
+        level_ids[:, None], slot_of[owner_rows]
+    ]
     new_weights = placed.reshape(count, paths * block, width)
     gate_new = contract(inputs, new_weights[0], 1, 1) * scale_d
     upper_new = contract(inputs, new_weights[1], 1, 1) * scale_d

time: 492 us -> 388 us (0.79)
  waiting for transfers between devices: 355 us -> 68.2 us
  Pallas kernels: 0 us -> 231 us
  local copies, waits for them, and re-layouts: 56.5 us -> 35.3 us
  matrix products: 37.9 us -> 22.1 us
  starting transfers between devices: 23.7 us -> 8.98 us
    all_to_all x2 -> x0, waiting for transfers between devices: 281 us -> none  [the longest x1 140 us: shards(): lax.all_to_all(blocks[jnp.arange(count)[:, None], inverse], 'path', split...]
    pallas_call x0 -> x1, Pallas kernels: none -> 231 us  [exchange(): pl.pallas_call(exchange_kernel, out_shape=(jax.ShapeDtypeStruct((LV, NX,...]
    all_to_all x2 -> x0, starting transfers between devices: 18.3 us -> none  [the longest x1 9.97 us: shards(): lax.all_to_all(blocks[jnp.arange(count)[:, None], inverse], 'path', split...]
    gather x5 -> x10, local copies, waits for them, and re-layouts: 38.7 us -> 22.2 us  [the longest x3 10.1 us: shards(): leaving = blocks[level_ids[:, None], inverse[:, ahead.reshape(-1)]]]
    dot_general x1 -> x0, matrix products: 14.2 us -> none  [shards(): jnp.einsum('lmp,lpbd->lmbd', table.astype(jnp.bfloat16), received, prefer...]
    all_gather x1, waiting for transfers between devices: 31.2 us -> 22.6 us  [shards(): lax.all_gather(tokens, 'mp', axis=1, tiled=True)]
    all_to_all x1 -> x0, local copies, waits for them, and re-layouts: 6.56 us -> none  [shards(): lax.all_to_all(leaving, 'path', split_axis=1, concat_axis=1, tiled=True)]
  transfers between devices with their start and end apart: 5 -> 3, of which waited for: 5 -> 3; matrix products, arithmetic and copies ran while one was open for 2% -> 4% of each run, Pallas kernels for 0% -> 0%
where the time goes in v2:
time: 388 us; the launch traced here: 387 us
  Pallas kernels  231 us (60%)
  waiting for transfers between devices  68.2 us (18%)
  local copies, waits for them, and re-layouts  35.3 us (9%)
  matrix products  22.1 us (6%)
  between operations  14.3 us (4%)
  starting transfers between devices  8.98 us (2%)
  other arithmetic  7.01 us (2%)
    pallas_call x1, Pallas kernels, exchange(): pl.pallas_call(exchange_kernel, out_shape=(jax.ShapeDtypeStruct((LV, NX,...  231 us
    all_gather x1, waiting for transfers between devices, shards(): lax.all_gather(cotangent, 'mp', axis=1, tiled=True)  23.6 us
    all_gather x1, waiting for transfers between devices, shards(): lax.all_gather(tokens, 'mp', axis=1, tiled=True)  22.6 us
    dot_general x8, matrix products, contract(): lax.dot_general(left, right, (((left_dim,), (right_dim,)), ((), ())), pre...  22.1 us
    all_to_all x1, waiting for transfers between devices, shards(): lax.all_to_all(slices, 'mp', split_axis=0, concat_axis=0, tiled=True)  20.6 us
    gather x3, local copies, waits for them, and re-layouts, shards(): leaving = blocks[level_ids[:, None], inverse[:, ahead.reshape(-1)]]  10.1 us
    gather x1, local copies, waits for them, and re-layouts, shards(): returned.reshape(count, paths, block, width)  9.43 us
    all_to_all x1, starting transfers between devices, shards(): lax.all_to_all(slices, 'mp', split_axis=0, concat_axis=0, tiled=True)  8.9 us
  transfers between devices with their start and end apart: 3, of which 3 were waited for; matrix products, arithmetic and copies ran while one was open for 4% of the time, Pallas kernels for 0%

profile of v2, /device:TPU:1, one launch (start us, length us, event | category | flops | bytes accessed | tf_op | source)
XLA Modules:
  0.0 387.2 jit_solution(7751399840569012929)
XLA Ops:
  8.7 0.8 convert_reduce_fusion
  9.4 0.9 fusion.43
  11.6 0.8 copy.33
  13.4 1.2 gather_fusion.5
  18.9 22.6 %all-gather.5.cloned.1.call-done = bf16[384,2048]{1,0:T(8,128)(2,1)} async-done(((bf16[384,256]{1,0:T(8,128)(2,1)}), bf16[384,2048]{1,0:T(8,128)(2,1)}) %all-gather.5.cloned.1.call-update) | async-done | bytes 1572880 | tf_op jit(solution)/shard_map/all_gather | solution.py:314
  41.5 3.2 fusion.9
  44.7 3.5 fusion.15
  48.2 23.6 %all-gather.3.cloned.1.call-done = bf16[384,2048]{1,0:T(8,128)(2,1)} async-done(((bf16[384,256]{1,0:T(8,128)(2,1)}), bf16[384,2048]{1,0:T(8,128)(2,1)}) %all-gather.3.cloned.1.call-update) | async-done | bytes 1572880 | tf_op jit(solution)/shard_map/all_gather | solution.py:315
  71.8 3.2 fusion.12
  75.1 3.1 subtract_convert_fusion
  78.3 1.5 subtract_convert_fusion.2
  79.8 1.4 subtract_convert_fusion.1
  81.1 3.3 pad_maximum_fusion
  84.4 9.4 %gather_fusion.4 = bf16[96,16,2048]{2,1,0:T(8,128)(2,1)} fusion(bf16[3,32,16,2048]{3,2,1,0:T(8,128)(2,1)} %pad_maximum_fusion, s32[96]{0:T(128)S(1)} %reshape.369), kind=kCustom, calls=%fused_computation.4 | custom fusion | bytes 12583680 | tf_op jit(solution)/shard_map/gather | solution.py:369
  93.8 231.4 %shard_map.95 = (bf16[3,4,8,16,2048]{4,3,2,1,0:T(8,128)(2,1)}, bf16[3,8,16,2048]{3,2,1,0:T(8,128)(2,1)}) custom-call(f32[768]{0:T(1024)} %reshape.338.mask, s32[96]{0:T(128)} %reshape.331.pick, f32[24]{0:T(128)} %div.25.rcp, bf16[3,4,8,16,2048]{4,3,2,1,0:T(8,128)(2,1)} %bitcast.80, f32[3,8,16,2048]{3,2,1,0:T(8,128)} %bitcast.82, ...), custom_call_target="tpu_custom_call" | custom-call | tf_op jit(solution)/shard_map/pallas_call | solution.py:291
  325.3 9.4 %gather_fusion.6 = bf16[96,16,2048]{2,1,0:T(8,128)(2,1)} fusion(bf16[3,32,16,2048]{3,2,1,0:T(8,128)(2,1)} %bitcast.81, s32[96]{0:T(128)S(1)} %reshape.383), kind=kCustom, calls=%fused_computation.6 | custom fusion | bytes 12583680 | tf_op jit(solution)/shard_map/gather | solution.py:381
  334.7 5.3 %fusion.56 = (bf16[32,16,2048]{2,1,0:T(8,128)(2,1)S(1)}, bf16[32,16,2048]{2,1,0:T(8,128)(2,1)S(1)}, bf16[32,16,2048]{2,1,0:T(8,128)(2,1)}) fusion(bf16[96,16,2048]{2,1,0:T(8,128)(2,1)} %gather_fusion.6), kind=kLoop, calls=%fused_computation.101 | loop fusion | bytes 12582912 | tf_op jit(solution)/shard_map/slice | solution.py:385
  340.0 1.0 fusion.19
  341.0 5.2 %multiply_convert_fusion = bf16[384,2048]{1,0:T(8,128)(2,1)} fusion(bf16[512,2048]{1,0:T(8,128)(2,1)} %bitcast.85, bf16[512,2048]{1,0:T(8,128)(2,1)S(1)} %bitcast.84, bf16[384,2048]{1,0:T(8,128)(2,1)} %all-gather.5.cloned.1.call-done, f32[384,512]{1,0:T(8,128)S(1)} %fusion.19), kind=kOutput, calls=%fused_computation.11 | convolution fusion | flops 1613561856 | bytes 8126464 | tf_op jit(solution)/shard_map/dot_general | solution.py:307
  346.2 2.7 copy.49
  348.8 8.9 %all-to-all-start = ((bf16[8,384,256]{2,1,0:T(8,128)(2,1)}), bf16[8,384,256]{2,1,0:T(8,128)(2,1)S(1)}, u32[]{:S(2)}, u32[]{:S(2)}) async-start(bf16[8,384,256]{2,1,0:T(8,128)(2,1)} %bitcast.79), calls=%async_computation | async-start | bytes 3145728 | tf_op jit(solution)/shard_map/all_to_all | solution.py:392
  357.7 20.6 %all-to-all-done = bf16[8,384,256]{2,1,0:T(8,128)(2,1)S(1)} async-done(((bf16[8,384,256]{2,1,0:T(8,128)(2,1)}), bf16[8,384,256]{2,1,0:T(8,128)(2,1)S(1)}, u32[]{:S(2)}, u32[]{:S(2)}) %all-to-all-start) | async-done | bytes 1572896 | tf_op jit(solution)/shard_map/all_to_all | solution.py:392
  378.3 0.9 reduce_sum.42
  379.2 1.1 copy.51
  (56 shorter events, 8.0 us)
Async XLA Ops:
  7.2 3.2 copy-start
  7.2 34.3 %all-gather.5.cloned.1.call-start = ((), (), s32[]{:S(2)}) async-start(), calls=%async_computation.2 | async-start | bytes 1769472 | tf_op jit(solution)/shard_map/all_gather | solution.py:314
  7.9 63.9 %all-gather.3.cloned.1.call-start = ((), (), s32[]{:S(2)}) async-start(), calls=%async_computation.1 | async-start | bytes 1769472 | tf_op jit(solution)/shard_map/all_gather | solution.py:315
  41.5 3.2 copy-start.2
  71.8 3.2 copy-start.4
  71.8 3.2 copy-start.5
  71.8 6.4 %slice-start = ((s8[6291456]{0:T(1024)(128)(4,1)}), s8[4194304]{0:T(1024)(128)(4,1)S(1)}, s32[]{:S(2)}) async-start(s8[6291456]{0:T(1024)(128)(4,1)} %bitcast.97), calls=%async_computation.3 | async-start | bytes 8388608
  75.1 3.2 slice-start.1
  334.7 5.3 %copy-start.3 = (bf16[384,2048]{1,0:T(8,128)(2,1)S(1)}, bf16[384,2048]{1,0:T(8,128)(2,1)}, u32[]{:S(2)}) copy-start(bf16[384,2048]{1,0:T(8,128)(2,1)} %all-gather.5.cloned.1.call-done) | copy-start | bytes 4718596
  348.8 30.4 %copy-start.1 = (bf16[3,8,16,2048]{3,2,1,0:T(8,128)(2,1)S(1)}, bf16[3,8,16,2048]{3,2,1,0:T(8,128)(2,1)}, u32[]{:S(2)}) copy-start(bf16[3,8,16,2048]{3,2,1,0:T(8,128)(2,1)} %get-tuple-element.5) | copy-start | bytes 4718596
  348.8 29.5 %all-to-all-start = ((bf16[8,384,256]{2,1,0:T(8,128)(2,1)}), bf16[8,384,256]{2,1,0:T(8,128)(2,1)S(1)}, u32[]{:S(2)}, u32[]{:S(2)}) async-start(bf16[8,384,256]{2,1,0:T(8,128)(2,1)} %bitcast.79), calls=%async_computation | async-start | bytes 3145728 | tf_op jit(solution)/shard_map/all_to_all | solution.py:392
Sparse Core Ops, SparseCore 0:
  9.8 31.6 all-gather.4
  43.3 28.4 all-gather.2

commit v3 on v2

v3 whole, which is shorter than its diff:
```python
import jax
import jax.numpy as jnp
from jax import lax
from jax.experimental import pallas as pl
from jax.experimental.pallas import tpu as pltpu
from jax.sharding import PartitionSpec as P

MESH = pl.DeviceIdType.MESH
D = 2048
FF = 4096
ROWS = 384
NX = 4
NZ = 8
NY = 4
NP = NX * NZ
NMP = 8
PART = D // NMP
KORD = (4, 3, 5, 2, 6, 1, 7, 0)
POS = {k: i for i, k in enumerate(KORD)}
GROUPS = ((0, 1), (1, 3), (3, 5), (5, 7), (7, 8))
M = 8
LV = 3
B = 16
HID = NP * B
HALF = D // 2
HROW = ROWS // 2
CH = 256
SIGN = (-1, 1)

mu_outer = 0.9
eta_outer = 0.7
lr_inner = 2.0
scale_d = D ** (-0.5)
scale_f = FF ** (-0.5)
f32 = jnp.float32
bf16 = jnp.bfloat16


def contract(left, right, left_dim, right_dim):
    return lax.dot_general(
        left, right, (((left_dim,), (right_dim,)), ((), ())), preferred_element_type=f32
    )


def step_kernel(
    assign, table, rcp, tokens, cotangent, weights, outer, momentum, out, refreshed, *scratch
):
    it = iter(scratch)
    take = lambda n: [next(it) for _ in range(n)]
    pairs = lambda: [take(2) for _ in range(LV)]
    X = take(LV)
    B0, B1o, B1f, T2, B2, B3 = (pairs() for _ in range(6))
    C1, C2, C3d, S2, C3s, S3, C4 = (pairs() for _ in range(7))
    Y, WR, O, F = take(LV), take(LV), take(LV), take(LV)
    xg, cg = take(2)
    A0, A1, A2 = take(3)
    hid, pre0, pre1, perm, G, h2 = take(6)
    N0, NS, NR, TS2, TE, TS1, TR = take(7)
    mask = next(it)
    xs, xr, zs, zr, ls, gs, gr, ts, tr = take(9)
    me = lax.axis_index("path")
    mp = lax.axis_index("mp")
    x, z = me // NZ, lax.rem(me, NZ)
    y, core = mp // 2, lax.rem(mp, 2)
    right = [lax.rem(x + dx, NX) * NZ + z for dx in range(NX)]
    along = [x * NZ + lax.rem(z + NZ + s, NZ) for s in SIGN]
    ycol = lambda dy: lax.rem(y + dy + NY, NY) * 2 + core
    up, down, mate = ycol(1), ycol(-1), y * 2 + 1 - core

    barrier = pltpu.get_barrier_semaphore()
    for other in right[1:] + along:
        pl.semaphore_signal(barrier, inc=1, device_id={"path": other}, device_id_type=MESH)
    for other in (up, down, mate):
        pl.semaphore_signal(barrier, inc=1, device_id={"mp": other}, device_id_type=MESH)

    started, zc, xc, loc = [], {}, {}, {}

    def local(key, src, dst, index):
        c = pltpu.make_async_copy(src, dst, ls.at[index])
        c.start()
        loc[key] = c

    def describe(src, dst, ssem, rsem, axis, other):
        return pltpu.make_async_remote_copy(
            src_ref=src, dst_ref=dst, send_sem=ssem, recv_sem=rsem,
            device_id={axis: other}, device_id_type=MESH,
        )

    def remote(key, keep, *rest):
        c = describe(*rest)
        c.start()
        started.append(c)
        keep[key] = c

    local("xg", tokens, xg.at[mp], 15)
    local("cg", cotangent, cg.at[mp], 16)
    for l in range(LV):
        local(("w", l), weights.at[l], WR[l], 12 + l)
        local(("o", l), outer.at[l], O[l], 6 + l)
        local(("v", l), momentum.at[l], F[l], 9 + l)
    pl.semaphore_wait(barrier, 8)

    def gsend(t, n, src, dst, other):
        remote(("g", t, n), zc, src, dst, gs.at[t, n], gr.at[t, n], "mp", other)

    def gwait(t, n, dst):
        describe(dst, dst, gs.at[t, n], gr.at[t, n], "mp", mate).wait_recv()

    both = ((tokens, xg), (cotangent, cg))
    first, second = pl.ds(0, HROW), pl.ds(HROW, HROW)
    for t, (src, g) in enumerate(both):
        gsend(t, 0, src, g.at[mp], up)
        gsend(t, 1, src, g.at[mp], down)
        gsend(t, 2, src, g.at[mp], mate)

    def masks(i, carry):
        l, rest = i // (NZ * NX), lax.rem(i, NZ * NX)
        j, r = rest // NX, lax.rem(rest, NX)
        a = assign[l * NP + lax.rem(x - r + NX, NX) * NZ + lax.rem(z + j, NZ)]
        for m in range(M):
            mask[i * M + m] = jnp.where(a == m, 1.0, 0.0).astype(f32)
        return carry

    lax.fori_loop(0, LV * NZ * NX, masks, 0)

    def relay(t):
        g = both[t][1]
        lo, hi, far = ycol(-1), ycol(1), ycol(2)
        gwait(t, 0, g.at[lo])
        gsend(t, 3, g.at[lo, first], g.at[lo, first], up)
        gsend(t, 4, g.at[lo], g.at[lo], mate)
        gwait(t, 1, g.at[hi])
        gsend(t, 5, g.at[hi, second], g.at[hi, second], down)
        gsend(t, 6, g.at[hi], g.at[hi], mate)
        gwait(t, 3, g.at[far, first])
        gwait(t, 5, g.at[far, second])
        gsend(t, 7, g.at[far], g.at[far], mate)

    def arrived(t):
        g = both[t][1]
        other = lambda dy: lax.rem(y + dy, NY) * 2 + 1 - core
        gwait(t, 2, g.at[other(0)])
        gwait(t, 4, g.at[other(3)])
        gwait(t, 6, g.at[other(1)])
        gwait(t, 7, g.at[other(2)])
        loc["xg" if t == 0 else "cg"].wait()

    def project(jobs, g):
        def body(j, carry):
            cols = pl.ds(pl.multiple_of(j * PART, PART), PART)
            for acc, w in jobs:
                part = contract(w[:, :, cols].reshape(HID, PART), g[j], 1, 1)
                acc[...] += part.reshape(NP, B, ROWS)
            return carry

        for acc, _ in jobs:
            acc[...] = jnp.zeros_like(acc)
        lax.fori_loop(0, NMP, body, 0)

    relay(0)
    loc["w", 0].wait()
    loc["w", 1].wait()
    loc["w", 2].wait()
    arrived(0)
    relay(1)
    project(((A0, WR[0]), (A1, WR[1])), xg)
    arrived(1)
    project(((A2, WR[2]),), cg)

    def nonlinear(i, carry):
        gate, upper, back = A0[i] * scale_d, A1[i] * scale_d, A2[i] * scale_f
        sig = jax.nn.sigmoid(gate)
        act = gate * sig
        hid[i] = (act * upper).astype(bf16)
        pre0[i] = (back * upper * sig * (1.0 + gate * (1.0 - sig))).astype(bf16)
        pre1[i] = (back * act).astype(bf16)
        return carry

    lax.fori_loop(0, NP, nonlinear, 0)

    def finals(l):
        left = (pre0, pre1, hid)[l]
        g = (xg, xg, cg)[l]
        rate = lr_inner * (scale_d, scale_d, scale_f)[l]

        def gather(s, carry):
            perm[s] = left[table[l * NP + s]]
            return carry

        lax.fori_loop(0, NP, gather, 0, unroll=4)

        def body(j, carry):
            cols = pl.ds(pl.multiple_of(j * PART, PART), PART)
            G[...] = contract(perm[...].reshape(HID, ROWS), g[j], 1, 0).reshape(NP, B, PART)

            def rows(s, inner):
                w = WR[l][table[l * NP + s], :, cols].astype(f32)
                Y[l][s, :, cols] = (w - rate * G[s]).astype(bf16)
                return inner

            return lax.fori_loop(0, NP, rows, carry, unroll=8)

        lax.fori_loop(0, NMP, body, 0)

    def zsend(l, s, step, src, dst):
        remote(
            (l, s, step), zc, src, dst, zs.at[l, s, step], zr.at[l, s, step], "path", along[s]
        )

    def zwait(l, s, step):
        zc[l, s, step].wait_recv()

    def xwait(l, g):
        for dx in range(1, NX):
            xc[l, g, dx].wait_recv()

    def combine(dst, bases, terms, lo, hi):
        def body(c, carry):
            col = pl.multiple_of(lo + c * CH, CH)
            vals = [
                (ref[idx, :, pl.ds(pl.multiple_of(col - off, CH), CH)].astype(f32), at)
                for ref, idx, off, at in terms
            ]
            for m in range(M):
                acc = None
                for base in bases:
                    v = base[m, :, pl.ds(col, CH)].astype(f32)
                    acc = v if acc is None else acc + v
                for v, at in vals:
                    t = v * mask[at + m]
                    acc = t if acc is None else acc + t
                dst(m, col, acc)
            return carry

        lax.fori_loop(0, (hi - lo) // CH, body, 0)

    def at(l, j, r):
        return ((l * NZ + j % NZ) * NX + r) * M

    def own(l, k):
        return [(X[l].at[POS[k % NZ]], r, 0, at(l, 0, r)) for r in range(NX)]

    def into(ref):
        def put(m, col, acc):
            ref[m, :, pl.ds(col, CH)] = acc.astype(bf16)
        return put

    def pick(l, j, dx):
        return assign[l * NP + lax.rem(x + dx, NX) * NZ + lax.rem(z + j % NZ, NZ)]

    def a0(l):
        local((l, "own"), Y[l].at[pl.ds(0, NZ)], X[l].at[:, 0], l)
        for g, (lo, hi) in enumerate(GROUPS):
            for dx in (1, 3, 2):
                remote(
                    (l, g, dx), xc, Y[l].at[pl.ds(dx * NZ + lo, hi - lo)],
                    X[l].at[pl.ds(lo, hi - lo), dx], xs.at[0, l, g, dx - 1], xr.at[0, l, g, dx - 1],
                    "path", right[dx],
                )

    def a1(l):
        loc[l, "own"].wait()
        xwait(l, 0)
        for s in (0, 1):
            zsend(l, s, 0, X[l].at[0, :, :, pl.ds(s * HALF, HALF)], B0[l][s])

    def a2(l):
        xwait(l, 1)
        for s in (0, 1):
            zsend(l, s, 1, X[l].at[POS[3 * SIGN[s] % NZ]], B1o[l][s])
        for s in (0, 1):
            zwait(l, s, 0)
            zsend(l, s, 2, B0[l][s], B1f[l][s])

    def a3(l):
        xwait(l, 2)
        for s in (0, 1):
            sg = SIGN[s]
            zwait(l, s, 1)
            near = own(l, 2 * sg) + [(B1o[l][s], r, 0, at(l, -sg, r)) for r in range(NX)]
            o = (1 - s) * HALF
            combine(into(T2[l][s]), [], near, o, o + HALF)
            zwait(l, s, 2)
            o = s * HALF
            far = [(B1f[l][s], r, o, at(l, -2 * sg, r)) for r in range(NX)]
            combine(into(T2[l][s]), [], near + far, o, o + HALF)
            zsend(l, s, 3, T2[l][s], B2[l][s])

    def a4(l):
        xwait(l, 3)
        for s in (0, 1):
            zwait(l, s, 3)
            combine(into(B2[l][s]), [B2[l][s]], own(l, SIGN[s]), 0, D)
            zsend(l, s, 4, B2[l][s], B3[l][s])

    def stage(l, k, src):
        i = POS[k % NZ]
        for dx in range(NX):
            src(dx * NZ + i, dx, pick(l, 0, dx))

    def xsend(l, g):
        lo, hi = GROUPS[g]
        n = hi - lo
        for dx in (1, 3, 2):
            part = pl.ds(dx * NZ + lo, n)
            remote(
                (l, g, dx, "r"), xc, Y[l].at[part], WR[l].at[part],
                xs.at[1, l, g, dx - 1], xr.at[1, l, g, dx - 1], "path", right[dx],
            )

    def a5(l):
        xwait(l, 4)
        loc["o", l].wait()
        loc["v", l].wait()
        for s in (0, 1):
            zwait(l, s, 4)

        def put(m, col, acc):
            cols = pl.ds(col, CH)
            stored = O[l][m, :, cols]
            delta = stored - acc * rcp[l * M + m]
            velocity = mu_outer * F[l][m, :, cols].astype(f32) + delta
            F[l][m, :, cols] = (stored - eta_outer * (delta + mu_outer * velocity)).astype(bf16)

        combine(put, [B3[l][0], B3[l][1]], own(l, 0), 0, D)
        for s in (0, 1):
            zsend(l, s, 5, F[l], C1[l][s])
        local((l, "fresh"), F[l], refreshed.at[l], 3 + l)
        for g in range(len(GROUPS)):
            for dx in range(1, NX):
                xc[l, g, dx].wait_send()

        def src(i, dx, a):
            Y[l][i] = F[l][a]

        stage(l, 0, src)
        xsend(l, 4)

    def a6(l):
        for s in (0, 1):
            zwait(l, s, 5)
            zsend(l, s, 6, C1[l][s], C2[l][s])
        for s in (0, 1):
            def src(i, dx, a):
                Y[l][i] = C1[l][s][a]

            stage(l, -SIGN[s], src)
        xsend(l, 3)

    def a7(l):
        for s in (0, 1):
            zwait(l, s, 6)
            zsend(l, s, 7, C2[l][s].at[:, :, pl.ds(s * HALF, HALF)], C3d[l][s])
            for dx in range(NX):
                S2[l][s][dx] = C2[l][s][pick(l, SIGN[s], dx), :, pl.ds((1 - s) * HALF, HALF)]
            zsend(l, s, 8, S2[l][s], C3s[l][s])
        for s in (0, 1):
            def src(i, dx, a):
                Y[l][i] = C2[l][s][a]

            stage(l, -2 * SIGN[s], src)
        xsend(l, 2)

    def a8(l):
        for s in (0, 1):
            zwait(l, s, 7)
            for dx in range(NX):
                S3[l][s][dx] = C3d[l][s][pick(l, SIGN[s], dx)]
            zsend(l, s, 9, S3[l][s], C4[l][s])
        for s in (0, 1):
            zwait(l, s, 8)

            def src(i, dx, a):
                Y[l][i, :, pl.ds(s * HALF, HALF)] = C3d[l][s][a]
                Y[l][i, :, pl.ds((1 - s) * HALF, HALF)] = C3s[l][s][dx]

            stage(l, -3 * SIGN[s], src)
        xsend(l, 1)

    def a9(l):
        for s in (0, 1):
            zwait(l, s, 9)

        def src(i, dx, a):
            for s in (0, 1):
                Y[l][i, :, pl.ds(s * HALF, HALF)] = C4[l][s][dx]

        stage(l, 4, src)
        xsend(l, 0)
        local((l, "mine"), Y[l].at[pl.ds(0, NZ)], WR[l].at[pl.ds(0, NZ)], 17 + l)

    def settle(l):
        for g in range(len(GROUPS)):
            for dx in range(1, NX):
                xc[l, g, dx, "r"].wait_recv()
        loc[l, "mine"].wait()

    def forward(l):
        settle(l)
        if l < 2:
            project((((A0, A1)[l], WR[l]),), xg)
        if l == 1:
            def body(s, carry):
                gate = A0[table[LV * NP + s]] * scale_d
                upper = A1[table[(LV + 1) * NP + s]] * scale_d
                A2[s] = gate * jax.nn.sigmoid(gate) * upper
                return carry

            lax.fori_loop(0, NP, body, 0)
            h2[...] = A2[...].reshape(HID, ROWS).T.astype(bf16)

    finals(0)
    a0(0)
    finals(1)
    steps = (a0, a1, a2, a3, a4, a5, a6, a7, a8, a9)
    for slot in range(1, len(steps) + LV - 1):
        for l in range(LV):
            if 0 <= slot - l < len(steps):
                steps[slot - l](l)
        if slot == 1:
            finals(2)
        if slot >= len(steps):
            forward(slot - len(steps))
    settle(2)

    def block(j):
        cols = pl.ds(pl.multiple_of(j * PART, PART), PART)
        return contract(h2[...], WR[2][:, :, cols].reshape(HID, PART), 1, 0) * scale_f

    def tsend(n, src, dst, other):
        remote(("t", n), zc, src, dst, ts.at[n], tr.at[n], "mp", other)

    for dy in (2, 1, 3, 0):
        NS[dy] = block(lax.rem(y + dy, NY) * 2 + 1 - core).astype(bf16)
        tsend(dy, NS.at[dy], NR.at[dy], mate)
    for dy in (2, 1, 3, 0):
        N0[dy] = block(ycol(dy))
    zc["t", 2].wait_recv()
    pair = N0[2] + NR[2].astype(f32)
    TS2[0] = pair[:HROW].astype(bf16)
    TS2[1] = pair[HROW:].astype(bf16)
    tsend(4, TS2.at[0], TE.at[0], up)
    tsend(5, TS2.at[1], TE.at[1], down)
    for s, dy, rows, rest in ((0, 1, first, second), (1, 3, second, first)):
        zc["t", dy].wait_recv()
        TS1[s, rest] = (N0[dy, rest] + NR[dy, rest].astype(f32)).astype(bf16)
        zc["t", 4 + s].wait_recv()
        TS1[s, rows] = (
            N0[dy, rows] + NR[dy, rows].astype(f32) + TE[s].astype(f32)
        ).astype(bf16)
        tsend(6 + s, TS1.at[s], TR.at[s], (up, down)[s])
    zc["t", 0].wait_recv()
    zc["t", 6].wait_recv()
    zc["t", 7].wait_recv()
    out[...] = (
        N0[0] + NR[0].astype(f32) + TR[0].astype(f32) + TR[1].astype(f32)
    ).astype(bf16)
    done = {id(xc[l, g, dx]) for l in range(LV) for g in range(5) for dx in range(1, NX)}
    for c in started:
        if id(c) not in done:
            c.wait_send()
    for l in range(LV):
        loc[l, "fresh"].wait()


def step(assign, table, rcp, tokens, cotangent, weights, outer, momentum):
    bf = lambda *shape: pltpu.VMEM(shape, bf16)
    fl = lambda *shape: pltpu.VMEM(shape, f32)
    dense, dense_half = bf(M, B, D), bf(M, B, HALF)
    four, four_half = bf(NX, B, D), bf(NX, B, HALF)
    pairs = lambda kind: [kind] * (2 * LV)
    scratch = [bf(NZ, NX, B, D)] * LV
    for kind in (four_half, four, four_half, dense, dense, dense):
        scratch += pairs(kind)
    for kind in (dense, dense, dense_half, four_half, four_half, four_half, four_half):
        scratch += pairs(kind)
    scratch += [bf(NP, B, D)] * (2 * LV)
    scratch += [fl(M, B, D)] * LV + [dense] * LV
    scratch += [bf(NMP, ROWS, PART)] * 2
    scratch += [fl(NP, B, ROWS)] * 3
    scratch += [bf(NP, B, ROWS)] * 4 + [fl(NP, B, PART), bf(ROWS, HID)]
    scratch += [fl(NY, ROWS, PART), bf(NY, ROWS, PART), bf(NY, ROWS, PART)]
    scratch += [bf(2, HROW, PART)] * 2 + [bf(2, ROWS, PART)] * 2
    scratch += [pltpu.SMEM((LV * NZ * NX * M,), f32)]
    dma = pltpu.SemaphoreType.DMA
    scratch += [dma((2, LV, 5, 3)), dma((2, LV, 5, 3)), dma((LV, 2, 10)), dma((LV, 2, 10))]
    scratch += [dma((20,)), dma((2, 8)), dma((2, 8)), dma((8,)), dma((8,))]
    smem = pl.BlockSpec(memory_space=pltpu.SMEM)
    anyw = pl.BlockSpec(memory_space=pl.ANY)
    return pl.pallas_call(
        step_kernel,
        out_shape=(
            jax.ShapeDtypeStruct((ROWS, PART), bf16),
            jax.ShapeDtypeStruct((LV, M, B, D), bf16),
        ),
        in_specs=[smem, smem, smem, anyw, anyw, anyw, anyw, anyw],
        out_specs=(pl.BlockSpec(memory_space=pltpu.VMEM), anyw),
        scratch_shapes=scratch,
        compiler_params=pltpu.CompilerParams(
            collective_id=0, has_side_effects=True, vmem_limit_bytes=67043328
        ),
    )(assign, table, rcp, tokens, cotangent, weights, outer, momentum)


def shards(tokens, cotangent, path_weights, outer_weights, momentum, assignment, owners):
    here = lax.axis_index("path")
    at_x, at_z = here // NZ, here % NZ
    module_ids = jnp.arange(M, dtype=jnp.int32)
    ids = jnp.arange(NP, dtype=jnp.int32)
    mine = jnp.sum(jnp.where(ids == here, assignment, 0), axis=1)
    rows = jnp.sum(jnp.where((mine[:, None] == module_ids)[:, :, None], owners, 0), axis=1)
    k = (rows % NZ - at_z) % NZ
    place = 2 * (4 - jnp.minimum(k, NZ - k)) - (k < 4).astype(jnp.int32)
    leave = (rows // NZ - at_x) % NX * NZ + place
    back = (at_x - rows // NZ) % NX * NZ + place
    piece = jnp.sum(jnp.where(leave[:, None, :] == ids[:, None], ids, 0), axis=2)
    match = back[2][None, :] == ids[:, None]
    partner = jnp.sum(jnp.where(match[None], back[:2, None, :], 0), axis=2)
    table = jnp.concatenate([piece.reshape(-1), partner.reshape(-1)])
    shares = jnp.sum((assignment[:, None, :] == module_ids[:, None]).astype(f32), axis=2)
    outputs, fresh = step(
        assignment.reshape(-1),
        table,
        (1.0 / shares).reshape(-1),
        tokens,
        cotangent,
        path_weights.reshape(LV, NP, B, D),
        outer_weights.reshape(LV, M, B, D),
        momentum.reshape(LV, M, B, D),
    )
    return (outputs, fresh.reshape(1, LV, M, 1, B, D))


def solution(mesh):
    return jax.shard_map(
        shards,
        mesh=mesh,
        in_specs=(
            P("path", "mp"),
            P("path", "mp"),
            P("path", None, "mp", None),
            P("path", None, None, "mp", None, None),
            P("path", None, None, "mp", None, None),
            P(),
            P(),
        ),
        out_specs=(P("path", "mp"), P("path", None, None, "mp", None, None)),
        check_vma=False,
    )
```

time: 388 us -> 293 us (0.76)
  waiting for transfers between devices: 68.2 us -> 0 us
  Pallas kernels: 231 us -> 282 us
  local copies, waits for them, and re-layouts: 35.3 us -> 6.42 us
  matrix products: 22.1 us -> 0 us
  between operations: 14.3 us -> 0.68 us
  starting transfers between devices: 8.98 us -> 0 us
    pallas_call x1, Pallas kernels: 231 us -> 282 us  [step(): pl.pallas_call(step_kernel, out_shape=(jax.ShapeDtypeStruct((ROWS, PART),...]
    all_gather x2 -> x0, waiting for transfers between devices: 46.2 us -> none  [the longest x1 23.6 us: shards(): lax.all_gather(cotangent, 'mp', axis=1, tiled=True)]
    gather x11 -> x0, local copies, waits for them, and re-layouts: 22.8 us -> none  [the longest x3 10.1 us: shards(): leaving = blocks[level_ids[:, None], inverse[:, ahead.reshape(-1)]]]
    dot_general x8 -> x0, matrix products: 22.1 us -> none  [contract(): lax.dot_general(left, right, (((left_dim,), (right_dim,)), ((), ())), pre...]
    all_to_all x1 -> x0, waiting for transfers between devices: 20.6 us -> none  [shards(): lax.all_to_all(slices, 'mp', split_axis=0, concat_axis=0, tiled=True)]
    all_to_all x1 -> x0, starting transfers between devices: 8.9 us -> none  [shards(): lax.all_to_all(slices, 'mp', split_axis=0, concat_axis=0, tiled=True)]
    slice x1 -> x2, local copies, waits for them, and re-layouts: 5.27 us -> 0.01 us  [the longest x1 0.01 us: shards(): match = back[2][None, :] == ids[:, None]]
  transfers between devices with their start and end apart: 3 -> 0, of which waited for: 3 -> 0; matrix products, arithmetic and copies ran while one was open for 4% -> 0% of each run, Pallas kernels for 0% -> 0%
where the time goes in v3:
time: 293 us; the launch traced here: 292 us
  Pallas kernels  282 us (96%)
  local copies, waits for them, and re-layouts  6.42 us (2%)
  other arithmetic  3.41 us (1%)
    pallas_call x1, Pallas kernels, step(): pl.pallas_call(step_kernel, out_shape=(jax.ShapeDtypeStruct((ROWS, PART),...  282 us

profile of v3, /device:TPU:1, one launch (start us, length us, event | category | flops | bytes accessed | tf_op | source)
XLA Modules:
  0.0 292.1 jit_solution(11653155418980236202)
XLA Ops:
  0.7 0.8 select_reduce_fusion.3
  1.5 0.1 iota_compare_fusion.3
  1.5 1.3 reshape.135.assign
  2.8 0.8 select_reduce_fusion.2
  3.6 0.8 convert_reduce_fusion
  4.4 0.6 div.37.rcp
  5.1 0.1 select_reduce_fusion
  5.2 0.1 reshape.136
  5.3 0.1 select_reduce_fusion.1
  5.4 0.1 reshape.137
  5.5 0.6 pad_add_fusion.table
  6.2 281.6 %shard_map.86 = (bf16[384,256]{1,0:T(8,128)(2,1)}, bf16[3,8,16,2048]{3,2,1,0:T(8,128)(2,1)}) custom-call(s32[96]{0:T(128)} %reshape.135.assign, s32[160]{0:T(256)} %pad_add_fusion.table, f32[24]{0:T(128)} %div.37.rcp, bf16[384,256]{1,0:T(8,128)(2,1)} %tokens.1, bf16[384,256]{1,0:T(8,128)(2,1)} %cotangent.1, bf16[3,32,16,2048]{3,2,1,0:T(8,128)(2,1)} %bitcast.8, ...), custom_call_target="tpu_custom_call" | custom-call | tf_op jit(solution)/shard_map/pallas_call | solution.py:490
  287.8 1.6 copy.13
  289.4 2.7 copy.14
  (7 shorter events, 0.1 us)

commit v4 on v3

--- a/solution.py
+++ b/solution.py
@@ -43,7 +43,7 @@
 
 
 def step_kernel(
-    assign, table, rcp, tokens, cotangent, weights, outer, momentum, out, refreshed, *scratch
+    assign, owners, tokens, cotangent, weights, outer, momentum, out, refreshed, *scratch
 ):
     it = iter(scratch)
     take = lambda n: [next(it) for _ in range(n)]
@@ -56,7 +56,7 @@
     A0, A1, A2 = take(3)
     hid, pre0, pre1, perm, G, h2 = take(6)
     N0, NS, NR, TS2, TE, TS1, TR = take(7)
-    mask = next(it)
+    mask, shares, table = take(3)
     xs, xr, zs, zr, ls, gs, gr, ts, tr = take(9)
     me = lax.axis_index("path")
     mp = lax.axis_index("mp")
@@ -107,65 +107,125 @@
         describe(dst, dst, gs.at[t, n], gr.at[t, n], "mp", mate).wait_recv()
 
     both = ((tokens, xg), (cotangent, cg))
-    first, second = pl.ds(0, HROW), pl.ds(HROW, HROW)
-    for t, (src, g) in enumerate(both):
-        gsend(t, 0, src, g.at[mp], up)
-        gsend(t, 1, src, g.at[mp], down)
+    halves = (pl.ds(0, HROW), pl.ds(HROW, HROW))
+    lo_y, hi_y, far_y = ycol(-1), ycol(1), ycol(2)
+
+    def offer(t):
+        src, g = both[t]
+        for n, h in ((0, 0), (8, 1)):
+            gsend(t, n, src.at[halves[h]], g.at[mp, halves[h]], up)
+            gsend(t, n + 1, src.at[halves[1 - h]], g.at[mp, halves[1 - h]], down)
         gsend(t, 2, src, g.at[mp], mate)
+
+    def relay(t):
+        g = both[t][1]
+        gwait(t, 0, g.at[lo_y, halves[0]])
+        gsend(t, 3, g.at[lo_y, halves[0]], g.at[lo_y, halves[0]], up)
+        gwait(t, 1, g.at[hi_y, halves[1]])
+        gsend(t, 5, g.at[hi_y, halves[1]], g.at[hi_y, halves[1]], down)
+
+    def share_near(t):
+        g = both[t][1]
+        gwait(t, 8, g.at[lo_y, halves[1]])
+        gsend(t, 4, g.at[lo_y], g.at[lo_y], mate)
+        gwait(t, 9, g.at[hi_y, halves[0]])
+        gsend(t, 6, g.at[hi_y], g.at[hi_y], mate)
+
+    def share_far(t):
+        g = both[t][1]
+        gwait(t, 3, g.at[far_y, halves[0]])
+        gwait(t, 5, g.at[far_y, halves[1]])
+        gsend(t, 7, g.at[far_y], g.at[far_y], mate)
+
+    def near_arrived(t):
+        g = both[t][1]
+        other = lambda dy: lax.rem(y + dy, NY) * 2 + 1 - core
+        loc["xg" if t == 0 else "cg"].wait()
+        gwait(t, 2, g.at[other(0)])
+        gwait(t, 4, g.at[other(3)])
+        gwait(t, 6, g.at[other(1)])
+
+    def far_arrived(t):
+        gwait(t, 7, both[t][1].at[lax.rem(y + 2, NY) * 2 + 1 - core])
+
+    def project(acc, w, g, lo=0, hi=NMP):
+        def body(i, carry):
+            k = i // 2
+            dy = k + k // 2 - 2 * (k // 3)
+            j = lax.rem(y + dy, NY) * 2 + lax.rem(core + i, 2)
+            cols = pl.ds(pl.multiple_of(j * PART, PART), PART)
+            part = contract(w[:, :, cols].reshape(HID, PART), g[j], 1, 1)
+            acc[...] += part.reshape(NP, B, ROWS)
+            return carry
+
+        if lo == 0:
+            acc[...] = jnp.zeros_like(acc)
+        lax.fori_loop(lo, hi, body, 0)
 
     def masks(i, carry):
         l, rest = i // (NZ * NX), lax.rem(i, NZ * NX)
         j, r = rest // NX, lax.rem(rest, NX)
-        a = assign[l * NP + lax.rem(x - r + NX, NX) * NZ + lax.rem(z + j, NZ)]
+        a = assign[l, lax.rem(x - r + NX, NX) * NZ + lax.rem(z + j, NZ)]
         for m in range(M):
             mask[i * M + m] = jnp.where(a == m, 1.0, 0.0).astype(f32)
         return carry
 
+    def count(l):
+        def body(p, totals):
+            a = assign[l, p]
+            return tuple(t + jnp.where(a == m, 1.0, 0.0) for m, t in enumerate(totals))
+
+        totals = lax.fori_loop(0, NP, body, (jnp.float32(0),) * M)
+        for m in range(M):
+            shares[l * M + m] = totals[m]
+
+    mine = [assign[l, me] for l in range(LV)]
+
+    def pieces(l):
+        def body(s, carry):
+            dx, i = s // NZ, lax.rem(s, NZ)
+            k = 4 + (i + 1) // 2 * (1 - 2 * lax.rem(i, 2))
+            path = lax.rem(x + dx, NX) * NZ + lax.rem(z + k, NZ)
+            found = jnp.int32(0)
+            for q in range(1, NP):
+                found = jnp.where(owners[l, mine[l], q] == path, q, found)
+            table[l * NP + s] = found
+            return carry
+
+        lax.fori_loop(0, NP, body, 0)
+
+    def partners(s, carry):
+        r, i = s // NZ, lax.rem(s, NZ)
+        q = table[2 * NP + lax.rem(NX - r, NX) * NZ + i]
+        for l in (0, 1):
+            o = owners[l, mine[l], q]
+            k = lax.rem(lax.rem(o, NZ) - z + NZ, NZ)
+            i = 2 * (4 - jnp.minimum(k, NZ - k)) - jnp.where(k < 4, 1, 0)
+            table[(LV + l) * NP + s] = lax.rem(x - o // NZ + NX, NX) * NZ + i
+        return carry
+
+    offer(0)
     lax.fori_loop(0, LV * NZ * NX, masks, 0)
-
-    def relay(t):
-        g = both[t][1]
-        lo, hi, far = ycol(-1), ycol(1), ycol(2)
-        gwait(t, 0, g.at[lo])
-        gsend(t, 3, g.at[lo, first], g.at[lo, first], up)
-        gsend(t, 4, g.at[lo], g.at[lo], mate)
-        gwait(t, 1, g.at[hi])
-        gsend(t, 5, g.at[hi, second], g.at[hi, second], down)
-        gsend(t, 6, g.at[hi], g.at[hi], mate)
-        gwait(t, 3, g.at[far, first])
-        gwait(t, 5, g.at[far, second])
-        gsend(t, 7, g.at[far], g.at[far], mate)
-
-    def arrived(t):
-        g = both[t][1]
-        other = lambda dy: lax.rem(y + dy, NY) * 2 + 1 - core
-        gwait(t, 2, g.at[other(0)])
-        gwait(t, 4, g.at[other(3)])
-        gwait(t, 6, g.at[other(1)])
-        gwait(t, 7, g.at[other(2)])
-        loc["xg" if t == 0 else "cg"].wait()
-
-    def project(jobs, g):
-        def body(j, carry):
-            cols = pl.ds(pl.multiple_of(j * PART, PART), PART)
-            for acc, w in jobs:
-                part = contract(w[:, :, cols].reshape(HID, PART), g[j], 1, 1)
-                acc[...] += part.reshape(NP, B, ROWS)
-            return carry
-
-        for acc, _ in jobs:
-            acc[...] = jnp.zeros_like(acc)
-        lax.fori_loop(0, NMP, body, 0)
-
     relay(0)
+    offer(1)
+    pieces(0)
+    share_near(0)
+    pieces(1)
+    share_far(0)
+    relay(1)
+    near_arrived(0)
+    far_arrived(0)
     loc["w", 0].wait()
+    project(A0, WR[0], xg)
+    share_near(1)
     loc["w", 1].wait()
+    project(A1, WR[1], xg)
+    share_far(1)
+    near_arrived(1)
     loc["w", 2].wait()
-    arrived(0)
-    relay(1)
-    project(((A0, WR[0]), (A1, WR[1])), xg)
-    arrived(1)
-    project(((A2, WR[2]),), cg)
+    project(A2, WR[2], cg, 0, 6)
+    far_arrived(1)
+    project(A2, WR[2], cg, 6, NMP)
 
     def nonlinear(i, carry):
         gate, upper, back = A0[i] * scale_d, A1[i] * scale_d, A2[i] * scale_f
@@ -178,27 +238,33 @@
 
     lax.fori_loop(0, NP, nonlinear, 0)
 
-    def finals(l):
+    def finals(l, lo, hi):
         left = (pre0, pre1, hid)[l]
         g = (xg, xg, cg)[l]
         rate = lr_inner * (scale_d, scale_d, scale_f)[l]
-
-        def gather(s, carry):
-            perm[s] = left[table[l * NP + s]]
+        n = (hi - lo) * NX
+
+        def slot(i):
+            return lax.rem(i, NX) * NZ + i // NX
+
+        def gather(i, carry):
+            perm[i] = left[table[l * NP + slot(i)]]
             return carry
 
-        lax.fori_loop(0, NP, gather, 0, unroll=4)
+        lax.fori_loop(lo * NX, hi * NX, gather, 0, unroll=4)
 
         def body(j, carry):
             cols = pl.ds(pl.multiple_of(j * PART, PART), PART)
-            G[...] = contract(perm[...].reshape(HID, ROWS), g[j], 1, 0).reshape(NP, B, PART)
-
-            def rows(s, inner):
+            rows = perm[pl.ds(lo * NX, n)].reshape(n * B, ROWS)
+            G[pl.ds(lo * NX, n)] = contract(rows, g[j], 1, 0).reshape(n, B, PART)
+
+            def rows(i, inner):
+                s = slot(i)
                 w = WR[l][table[l * NP + s], :, cols].astype(f32)
-                Y[l][s, :, cols] = (w - rate * G[s]).astype(bf16)
+                Y[l][s, :, cols] = (w - rate * G[i]).astype(bf16)
                 return inner
 
-            return lax.fori_loop(0, NP, rows, carry, unroll=8)
+            return lax.fori_loop(lo * NX, hi * NX, rows, carry, unroll=4)
 
         lax.fori_loop(0, NMP, body, 0)
 
@@ -246,11 +312,11 @@
         return put
 
     def pick(l, j, dx):
-        return assign[l * NP + lax.rem(x + dx, NX) * NZ + lax.rem(z + j % NZ, NZ)]
-
-    def a0(l):
-        local((l, "own"), Y[l].at[pl.ds(0, NZ)], X[l].at[:, 0], l)
-        for g, (lo, hi) in enumerate(GROUPS):
+        return assign[l, lax.rem(x + dx, NX) * NZ + lax.rem(z + j % NZ, NZ)]
+
+    def send(l, *groups):
+        for g in groups:
+            lo, hi = GROUPS[g]
             for dx in (1, 3, 2):
                 remote(
                     (l, g, dx), xc, Y[l].at[pl.ds(dx * NZ + lo, hi - lo)],
@@ -258,32 +324,42 @@
                     "path", right[dx],
                 )
 
+    def keep(l):
+        local((l, "own"), Y[l].at[pl.ds(0, NZ)], X[l].at[:, 0], l)
+
     def a1(l):
         loc[l, "own"].wait()
         xwait(l, 0)
         for s in (0, 1):
             zsend(l, s, 0, X[l].at[0, :, :, pl.ds(s * HALF, HALF)], B0[l][s])
 
-    def a2(l):
+    def a2r(l):
         xwait(l, 1)
         for s in (0, 1):
             zsend(l, s, 1, X[l].at[POS[3 * SIGN[s] % NZ]], B1o[l][s])
+
+    def a2f(l):
         for s in (0, 1):
             zwait(l, s, 0)
             zsend(l, s, 2, B0[l][s], B1f[l][s])
 
-    def a3(l):
+    def near(l, s):
+        sg = SIGN[s]
+        return own(l, 2 * sg) + [(B1o[l][s], r, 0, at(l, -sg, r)) for r in range(NX)]
+
+    def a3n(l):
         xwait(l, 2)
         for s in (0, 1):
-            sg = SIGN[s]
             zwait(l, s, 1)
-            near = own(l, 2 * sg) + [(B1o[l][s], r, 0, at(l, -sg, r)) for r in range(NX)]
             o = (1 - s) * HALF
-            combine(into(T2[l][s]), [], near, o, o + HALF)
+            combine(into(T2[l][s]), [], near(l, s), o, o + HALF)
+
+    def a3f(l):
+        for s in (0, 1):
             zwait(l, s, 2)
             o = s * HALF
-            far = [(B1f[l][s], r, o, at(l, -2 * sg, r)) for r in range(NX)]
-            combine(into(T2[l][s]), [], near + far, o, o + HALF)
+            far = [(B1f[l][s], r, o, at(l, -2 * SIGN[s], r)) for r in range(NX)]
+            combine(into(T2[l][s]), [], near(l, s) + far, o, o + HALF)
             zsend(l, s, 3, T2[l][s], B2[l][s])
 
     def a4(l):
@@ -318,7 +394,7 @@
         def put(m, col, acc):
             cols = pl.ds(col, CH)
             stored = O[l][m, :, cols]
-            delta = stored - acc * rcp[l * M + m]
+            delta = stored - acc / shares[l * M + m]
             velocity = mu_outer * F[l][m, :, cols].astype(f32) + delta
             F[l][m, :, cols] = (stored - eta_outer * (delta + mu_outer * velocity)).astype(bf16)
 
@@ -398,7 +474,7 @@
     def forward(l):
         settle(l)
         if l < 2:
-            project((((A0, A1)[l], WR[l]),), xg)
+            project((A0, A1)[l], WR[l], xg)
         if l == 1:
             def body(s, carry):
                 gate = A0[table[LV * NP + s]] * scale_d
@@ -409,18 +485,60 @@
             lax.fori_loop(0, NP, body, 0)
             h2[...] = A2[...].reshape(HID, ROWS).T.astype(bf16)
 
-    finals(0)
-    a0(0)
-    finals(1)
-    steps = (a0, a1, a2, a3, a4, a5, a6, a7, a8, a9)
-    for slot in range(1, len(steps) + LV - 1):
-        for l in range(LV):
-            if 0 <= slot - l < len(steps):
-                steps[slot - l](l)
-        if slot == 1:
-            finals(2)
-        if slot >= len(steps):
-            forward(slot - len(steps))
+    finals(0, 0, 1)
+    send(0, 0)
+    finals(0, 1, NZ)
+    send(0, 1, 2)
+    keep(0)
+    a1(0)
+    finals(1, 0, NZ)
+    send(1, 0, 1)
+    send(0, 3, 4)
+    keep(1)
+    a2r(0)
+    a2f(0)
+    pieces(2)
+    finals(2, 0, NZ)
+    send(1, 2)
+    send(2, 0, 1)
+    send(1, 3, 4)
+    send(2, 2, 3, 4)
+    keep(2)
+    a3n(0)
+    a1(1)
+    a3f(0)
+    a2r(1)
+    a2f(1)
+    for l in range(LV):
+        count(l)
+    lax.fori_loop(0, NP, partners, 0)
+    a4(0)
+    a3n(1)
+    a3f(1)
+    a1(2)
+    a2r(2)
+    a2f(2)
+    a5(0)
+    a4(1)
+    a3n(2)
+    a3f(2)
+    a6(0)
+    a5(1)
+    a4(2)
+    a7(0)
+    a6(1)
+    a5(2)
+    a8(0)
+    a7(1)
+    a6(2)
+    a9(0)
+    a8(1)
+    a7(2)
+    forward(0)
+    a9(1)
+    a8(2)
+    forward(1)
+    a9(2)
     settle(2)
 
     def block(j):
@@ -441,7 +559,7 @@
     TS2[1] = pair[HROW:].astype(bf16)
     tsend(4, TS2.at[0], TE.at[0], up)
     tsend(5, TS2.at[1], TE.at[1], down)
-    for s, dy, rows, rest in ((0, 1, first, second), (1, 3, second, first)):
+    for s, dy, rows, rest in ((0, 1, *halves), (1, 3, *halves[::-1])):
         zc["t", dy].wait_recv()
         TS1[s, rest] = (N0[dy, rest] + NR[dy, rest].astype(f32)).astype(bf16)
         zc["t", 4 + s].wait_recv()
@@ -463,7 +581,7 @@
         loc[l, "fresh"].wait()
 
 
-def step(assign, table, rcp, tokens, cotangent, weights, outer, momentum):
+def step(assign, owners, tokens, cotangent, weights, outer, momentum):
     bf = lambda *shape: pltpu.VMEM(shape, bf16)
     fl = lambda *shape: pltpu.VMEM(shape, f32)
     dense, dense_half = bf(M, B, D), bf(M, B, HALF)
@@ -481,10 +599,11 @@
     scratch += [bf(NP, B, ROWS)] * 4 + [fl(NP, B, PART), bf(ROWS, HID)]
     scratch += [fl(NY, ROWS, PART), bf(NY, ROWS, PART), bf(NY, ROWS, PART)]
     scratch += [bf(2, HROW, PART)] * 2 + [bf(2, ROWS, PART)] * 2
-    scratch += [pltpu.SMEM((LV * NZ * NX * M,), f32)]
+    scratch += [pltpu.SMEM((LV * NZ * NX * M,), f32), pltpu.SMEM((LV * M,), f32)]
+    scratch += [pltpu.SMEM(((LV + 2) * NP,), jnp.int32)]
     dma = pltpu.SemaphoreType.DMA
     scratch += [dma((2, LV, 5, 3)), dma((2, LV, 5, 3)), dma((LV, 2, 10)), dma((LV, 2, 10))]
-    scratch += [dma((20,)), dma((2, 8)), dma((2, 8)), dma((8,)), dma((8,))]
+    scratch += [dma((20,)), dma((2, 10)), dma((2, 10)), dma((8,)), dma((8,))]
     smem = pl.BlockSpec(memory_space=pltpu.SMEM)
     anyw = pl.BlockSpec(memory_space=pl.ANY)
     return pl.pallas_call(
@@ -493,35 +612,19 @@
             jax.ShapeDtypeStruct((ROWS, PART), bf16),
             jax.ShapeDtypeStruct((LV, M, B, D), bf16),
         ),
-        in_specs=[smem, smem, smem, anyw, anyw, anyw, anyw, anyw],
+        in_specs=[smem, smem, anyw, anyw, anyw, anyw, anyw],
         out_specs=(pl.BlockSpec(memory_space=pltpu.VMEM), anyw),
         scratch_shapes=scratch,
         compiler_params=pltpu.CompilerParams(
             collective_id=0, has_side_effects=True, vmem_limit_bytes=67043328
         ),
-    )(assign, table, rcp, tokens, cotangent, weights, outer, momentum)
+    )(assign, owners, tokens, cotangent, weights, outer, momentum)
 
 
 def shards(tokens, cotangent, path_weights, outer_weights, momentum, assignment, owners):
-    here = lax.axis_index("path")
-    at_x, at_z = here // NZ, here % NZ
-    module_ids = jnp.arange(M, dtype=jnp.int32)
-    ids = jnp.arange(NP, dtype=jnp.int32)
-    mine = jnp.sum(jnp.where(ids == here, assignment, 0), axis=1)
-    rows = jnp.sum(jnp.where((mine[:, None] == module_ids)[:, :, None], owners, 0), axis=1)
-    k = (rows % NZ - at_z) % NZ
-    place = 2 * (4 - jnp.minimum(k, NZ - k)) - (k < 4).astype(jnp.int32)
-    leave = (rows // NZ - at_x) % NX * NZ + place
-    back = (at_x - rows // NZ) % NX * NZ + place
-    piece = jnp.sum(jnp.where(leave[:, None, :] == ids[:, None], ids, 0), axis=2)
-    match = back[2][None, :] == ids[:, None]
-    partner = jnp.sum(jnp.where(match[None], back[:2, None, :], 0), axis=2)
-    table = jnp.concatenate([piece.reshape(-1), partner.reshape(-1)])
-    shares = jnp.sum((assignment[:, None, :] == module_ids[:, None]).astype(f32), axis=2)
     outputs, fresh = step(
-        assignment.reshape(-1),
-        table,
-        (1.0 / shares).reshape(-1),
+        assignment,
+        owners,
         tokens,
         cotangent,
         path_weights.reshape(LV, NP, B, D),

time: 293 us -> 274 us (0.935)
  Pallas kernels: 282 us -> 268 us
  other arithmetic: 3.41 us -> 0 us
    pallas_call x1, Pallas kernels: 282 us -> 268 us  [step(): pl.pallas_call(step_kernel, out_shape=(jax.ShapeDtypeStruct((ROWS, PART),...]
where the time goes in v4:
time: 274 us; the launch traced here: 273 us
  Pallas kernels  268 us (98%)
  local copies, waits for them, and re-layouts  4.34 us (2%)
    pallas_call x1, Pallas kernels, step(): pl.pallas_call(step_kernel, out_shape=(jax.ShapeDtypeStruct((ROWS, PART),...  268 us

profile of v4, /device:TPU:1, one launch (start us, length us, event | category | flops | bytes accessed | tf_op | source)
XLA Modules:
  0.0 273.3 jit_solution(3003596969440387126)
XLA Ops:
  0.6 268.3 %shard_map.86 = (bf16[384,256]{1,0:T(8,128)(2,1)}, bf16[3,8,16,2048]{3,2,1,0:T(8,128)(2,1)}) custom-call(s32[3,32]{1,0:T(4,128)} %assign.1, s32[3,8,32]{2,1,0:T(8,128)} %owners.1, bf16[384,256]{1,0:T(8,128)(2,1)} %tokens.1, bf16[384,256]{1,0:T(8,128)(2,1)} %cotangent.1, bf16[3,32,16,2048]{3,2,1,0:T(8,128)(2,1)} %bitcast.6, f32[3,8,16,2048]{3,2,1,0:T(8,128)} %bitcast.7, ...), custom_call_target="tpu_custom_call" | custom-call | tf_op jit(solution)/shard_map/pallas_call | solution.py:609
  269.0 1.6 copy.12
  270.6 2.7 copy.13

commit v5 on v4

--- a/solution.py
+++ b/solution.py
@@ -537,8 +537,8 @@
     forward(0)
     a9(1)
     a8(2)
+    a9(2)
     forward(1)
-    a9(2)
     settle(2)
 
     def block(j):
@@ -548,28 +548,39 @@
     def tsend(n, src, dst, other):
         remote(("t", n), zc, src, dst, ts.at[n], tr.at[n], "mp", other)
 
-    for dy in (2, 1, 3, 0):
+    def give(dy):
         NS[dy] = block(lax.rem(y + dy, NY) * 2 + 1 - core).astype(bf16)
         tsend(dy, NS.at[dy], NR.at[dy], mate)
-    for dy in (2, 1, 3, 0):
+
+    def hold(dy):
         N0[dy] = block(ycol(dy))
+
+    sides = ((0, 1, *halves), (1, 3, *halves[::-1]))
+    for dy in (2, 1, 3):
+        give(dy)
+    hold(2)
+    hold(1)
     zc["t", 2].wait_recv()
     pair = N0[2] + NR[2].astype(f32)
     TS2[0] = pair[:HROW].astype(bf16)
     TS2[1] = pair[HROW:].astype(bf16)
     tsend(4, TS2.at[0], TE.at[0], up)
     tsend(5, TS2.at[1], TE.at[1], down)
-    for s, dy, rows, rest in ((0, 1, *halves), (1, 3, *halves[::-1])):
+    hold(3)
+    for s, dy, rows, rest in sides:
         zc["t", dy].wait_recv()
         TS1[s, rest] = (N0[dy, rest] + NR[dy, rest].astype(f32)).astype(bf16)
+        tsend(6 + s, TS1.at[s, rest], TR.at[s, rest], (up, down)[s])
+    give(0)
+    hold(0)
+    for s, dy, rows, rest in sides:
         zc["t", 4 + s].wait_recv()
         TS1[s, rows] = (
             N0[dy, rows] + NR[dy, rows].astype(f32) + TE[s].astype(f32)
         ).astype(bf16)
-        tsend(6 + s, TS1.at[s], TR.at[s], (up, down)[s])
-    zc["t", 0].wait_recv()
-    zc["t", 6].wait_recv()
-    zc["t", 7].wait_recv()
+        tsend(8 + s, TS1.at[s, rows], TR.at[s, rows], (up, down)[s])
+    for n in (0, 6, 7, 8, 9):
+        zc["t", n].wait_recv()
     out[...] = (
         N0[0] + NR[0].astype(f32) + TR[0].astype(f32) + TR[1].astype(f32)
     ).astype(bf16)
@@ -603,7 +614,7 @@
     scratch += [pltpu.SMEM(((LV + 2) * NP,), jnp.int32)]
     dma = pltpu.SemaphoreType.DMA
     scratch += [dma((2, LV, 5, 3)), dma((2, LV, 5, 3)), dma((LV, 2, 10)), dma((LV, 2, 10))]
-    scratch += [dma((20,)), dma((2, 10)), dma((2, 10)), dma((8,)), dma((8,))]
+    scratch += [dma((20,)), dma((2, 10)), dma((2, 10)), dma((10,)), dma((10,))]
     smem = pl.BlockSpec(memory_space=pltpu.SMEM)
     anyw = pl.BlockSpec(memory_space=pl.ANY)
     return pl.pallas_call(
@@ -621,6 +632,36 @@
     )(assign, owners, tokens, cotangent, weights, outer, momentum)
 
 
+def place_kernel(o, r, out, refreshed, ov, rv, sin, sout):
+    parts = [(o, ov, out)] + [(r.at[l], rv.at[l], refreshed.at[l]) for l in range(LV)]
+    first = [pltpu.make_async_copy(a, v, sin.at[i]) for i, (a, v, b) in enumerate(parts)]
+    last = [pltpu.make_async_copy(v, b, sout.at[i]) for i, (a, v, b) in enumerate(parts)]
+    for c in first:
+        c.start()
+    for c, d in zip(first, last):
+        c.wait()
+        d.start()
+    for d in last:
+        d.wait()
+
+
+def place(o, r):
+    anyw = pl.BlockSpec(memory_space=pl.ANY)
+    dma = pltpu.SemaphoreType.DMA
+    return pl.pallas_call(
+        place_kernel,
+        out_shape=(jax.ShapeDtypeStruct(o.shape, bf16), jax.ShapeDtypeStruct(r.shape, bf16)),
+        in_specs=[anyw, anyw],
+        out_specs=(anyw, anyw),
+        scratch_shapes=[
+            pltpu.VMEM(o.shape, bf16),
+            pltpu.VMEM(r.shape, bf16),
+            dma((1 + LV,)),
+            dma((1 + LV,)),
+        ],
+    )(o, r)
+
+
 def shards(tokens, cotangent, path_weights, outer_weights, momentum, assignment, owners):
     outputs, fresh = step(
         assignment,
@@ -631,6 +672,7 @@
         outer_weights.reshape(LV, M, B, D),
         momentum.reshape(LV, M, B, D),
     )
+    outputs, fresh = place(outputs, fresh)
     return (outputs, fresh.reshape(1, LV, M, 1, B, D))
 
 

time: 274 us -> 272 us (level)
  local copies, waits for them, and re-layouts: 4.34 us -> 0 us
  Pallas kernels: 268 us -> 271 us
    unnamed x2 -> x0, local copies, waits for them, and re-layouts: 4.34 us -> none
where the time goes in v5:
time: 272 us; the launch traced here: 271 us
  Pallas kernels  271 us (100%)
    pallas_call x1, Pallas kernels, step(): pl.pallas_call(step_kernel, out_shape=(jax.ShapeDtypeStruct((ROWS, PART),...  268 us

profile of v5, /device:TPU:1, one launch (start us, length us, event | category | flops | bytes accessed | tf_op | source)
XLA Modules:
  0.0 271.4 jit_solution(7561517270183474051)
XLA Ops:
  0.6 268.4 %shard_map.86 = (bf16[384,256]{1,0:T(8,128)(2,1)}, bf16[3,8,16,2048]{3,2,1,0:T(8,128)(2,1)}) custom-call(s32[3,32]{1,0:T(4,128)} %assign.1, s32[3,8,32]{2,1,0:T(8,128)} %owners.1, bf16[384,256]{1,0:T(8,128)(2,1)} %tokens.1, bf16[384,256]{1,0:T(8,128)(2,1)} %cotangent.1, bf16[3,32,16,2048]{3,2,1,0:T(8,128)(2,1)} %bitcast.6, f32[3,8,16,2048]{3,2,1,0:T(8,128)} %bitcast.7, ...), custom_call_target="tpu_custom_call" | custom-call | tf_op jit(solution)/shard_map/pallas_call | solution.py:620
  269.1 2.4 shard_map.87

commit v6 on v5

--- a/solution.py
+++ b/solution.py
@@ -49,13 +49,13 @@
     take = lambda n: [next(it) for _ in range(n)]
     pairs = lambda: [take(2) for _ in range(LV)]
     X = take(LV)
-    B0, B1o, B1f, T2, B2, B3 = (pairs() for _ in range(6))
+    B0, B1o, B1f, X1o, X1f, T2, B2, B3 = (pairs() for _ in range(8))
     C1, C2, C3d, S2, C3s, S3, C4 = (pairs() for _ in range(7))
     Y, WR, O, F = take(LV), take(LV), take(LV), take(LV)
     xg, cg = take(2)
     A0, A1, A2 = take(3)
-    hid, pre0, pre1, perm, G, h2 = take(6)
-    N0, NS, NR, TS2, TE, TS1, TR = take(7)
+    hid, pre0, pre1, perm, G, h2, h2b = take(7)
+    N0, N1, NS, NR, TS2, TE, TS1, TR = take(8)
     mask, shares, table = take(3)
     xs, xr, zs, zr, ls, gs, gr, ts, tr = take(9)
     me = lax.axis_index("path")
@@ -304,7 +304,7 @@
         return ((l * NZ + j % NZ) * NX + r) * M
 
     def own(l, k):
-        return [(X[l].at[POS[k % NZ]], r, 0, at(l, 0, r)) for r in range(NX)]
+        return [(X[l].at[POS[k % NZ] - 3], r, 0, at(l, 0, r)) for r in range(NX)]
 
     def into(ref):
         def put(m, col, acc):
@@ -320,45 +320,71 @@
             for dx in (1, 3, 2):
                 remote(
                     (l, g, dx), xc, Y[l].at[pl.ds(dx * NZ + lo, hi - lo)],
-                    X[l].at[pl.ds(lo, hi - lo), dx], xs.at[0, l, g, dx - 1], xr.at[0, l, g, dx - 1],
+                    X[l].at[pl.ds(lo - 3, hi - lo), dx], xs.at[0, l, g, dx - 1], xr.at[0, l, g, dx - 1],
                     "path", right[dx],
                 )
 
     def keep(l):
-        local((l, "own"), Y[l].at[pl.ds(0, NZ)], X[l].at[:, 0], l)
-
-    def a1(l):
-        loc[l, "own"].wait()
-        xwait(l, 0)
-        for s in (0, 1):
-            zsend(l, s, 0, X[l].at[0, :, :, pl.ds(s * HALF, HALF)], B0[l][s])
-
-    def a2r(l):
-        xwait(l, 1)
-        for s in (0, 1):
-            zsend(l, s, 1, X[l].at[POS[3 * SIGN[s] % NZ]], B1o[l][s])
+        local((l, "own"), Y[l].at[pl.ds(3, NZ - 3)], X[l].at[:, 0], l)
+
+    def early4(l):
+        for dx in range(NX):
+            for s in (0, 1):
+                half = pl.ds(s * HALF, HALF)
+                zsend(l, s, 10 + dx, Y[l].at[dx * NZ, :, half], B0[l][s].at[dx])
+
+    def early3(l):
+        for dx in range(NX):
+            for s in (0, 1):
+                zsend(l, s, 14 + dx, Y[l].at[dx * NZ + POS[3 * SIGN[s] % NZ]], B1o[l][s].at[dx])
 
     def a2f(l):
         for s in (0, 1):
-            zwait(l, s, 0)
+            for dx in range(NX):
+                zwait(l, s, 10 + dx)
             zsend(l, s, 2, B0[l][s], B1f[l][s])
+
+    def axn(l):
+        for s in (0, 1):
+            for dx in range(NX):
+                zwait(l, s, 14 + dx)
+            for dx in (1, 3, 2):
+                remote(
+                    (l, "o", s, dx), xc, B1o[l][s].at[dx], X1o[l][s].at[dx],
+                    xs.at[0, l, s, dx - 1], xr.at[0, l, s, dx - 1], "path", right[dx],
+                )
+
+    def axf(l):
+        for s in (0, 1):
+            zwait(l, s, 2)
+            for dx in (1, 3, 2):
+                remote(
+                    (l, "f", s, dx), xc, B1f[l][s].at[dx], X1f[l][s].at[dx],
+                    xs.at[2, l, s, dx - 1], xr.at[2, l, s, dx - 1], "path", right[dx],
+                )
 
     def near(l, s):
         sg = SIGN[s]
-        return own(l, 2 * sg) + [(B1o[l][s], r, 0, at(l, -sg, r)) for r in range(NX)]
+        terms = [(B1o[l][s], 0, 0, at(l, -sg, 0))]
+        terms += [(X1o[l][s], r, 0, at(l, -sg, r)) for r in range(1, NX)]
+        return own(l, 2 * sg) + terms
 
     def a3n(l):
+        loc[l, "own"].wait()
         xwait(l, 2)
         for s in (0, 1):
-            zwait(l, s, 1)
+            for dx in range(1, NX):
+                xc[l, "o", s, dx].wait_recv()
             o = (1 - s) * HALF
             combine(into(T2[l][s]), [], near(l, s), o, o + HALF)
 
     def a3f(l):
         for s in (0, 1):
-            zwait(l, s, 2)
+            for dx in range(1, NX):
+                xc[l, "f", s, dx].wait_recv()
             o = s * HALF
-            far = [(B1f[l][s], r, o, at(l, -2 * SIGN[s], r)) for r in range(NX)]
+            far = [(B1f[l][s], 0, o, at(l, -2 * SIGN[s], 0))]
+            far += [(X1f[l][s], r, o, at(l, -2 * SIGN[s], r)) for r in range(1, NX)]
             combine(into(T2[l][s]), [], near(l, s) + far, o, o + HALF)
             zsend(l, s, 3, T2[l][s], B2[l][s])
 
@@ -402,9 +428,12 @@
         for s in (0, 1):
             zsend(l, s, 5, F[l], C1[l][s])
         local((l, "fresh"), F[l], refreshed.at[l], 3 + l)
-        for g in range(len(GROUPS)):
+        for g in range(2, len(GROUPS)):
             for dx in range(1, NX):
                 xc[l, g, dx].wait_send()
+        for s in (0, 1):
+            for n in range(10, 18):
+                zc[l, s, n].wait_send()
 
         def src(i, dx, a):
             Y[l][i] = F[l][a]
@@ -465,59 +494,72 @@
         xsend(l, 0)
         local((l, "mine"), Y[l].at[pl.ds(0, NZ)], WR[l].at[pl.ds(0, NZ)], 17 + l)
 
-    def settle(l):
-        for g in range(len(GROUPS)):
+    def settle(l, first=0, last=len(GROUPS)):
+        for g in range(first, last):
             for dx in range(1, NX):
                 xc[l, g, dx, "r"].wait_recv()
-        loc[l, "mine"].wait()
+        if last == len(GROUPS):
+            loc[l, "mine"].wait()
 
     def forward(l):
         settle(l)
         if l < 2:
             project((A0, A1)[l], WR[l], xg)
         if l == 1:
-            def body(s, carry):
+            def unit(i, s):
                 gate = A0[table[LV * NP + s]] * scale_d
                 upper = A1[table[(LV + 1) * NP + s]] * scale_d
-                A2[s] = gate * jax.nn.sigmoid(gate) * upper
+                A2[i] = gate * jax.nn.sigmoid(gate) * upper
+
+            def body(i, carry):
+                unit(i, i // (NZ - 1) * NZ + 1 + lax.rem(i, NZ - 1))
                 return carry
 
-            lax.fori_loop(0, NP, body, 0)
-            h2[...] = A2[...].reshape(HID, ROWS).T.astype(bf16)
+            lax.fori_loop(0, NP - NX, body, 0)
+            for dx in range(NX):
+                unit(NP - NX + dx, dx * NZ)
+            h2[...] = A2[: NP - NX].reshape(HID - NX * B, ROWS).T.astype(bf16)
+            h2b[...] = A2[NP - NX :].reshape(NX * B, ROWS).T.astype(bf16)
 
     finals(0, 0, 1)
-    send(0, 0)
+    early4(0)
     finals(0, 1, NZ)
-    send(0, 1, 2)
+    early3(0)
+    send(0, 2)
     keep(0)
-    a1(0)
+    a2f(0)
     finals(1, 0, NZ)
-    send(1, 0, 1)
-    send(0, 3, 4)
+    early4(1)
+    early3(1)
     keep(1)
-    a2r(0)
-    a2f(0)
+    axn(0)
     pieces(2)
+    axf(0)
+    send(0, 3)
+    send(1, 2)
     finals(2, 0, NZ)
-    send(1, 2)
-    send(2, 0, 1)
-    send(1, 3, 4)
-    send(2, 2, 3, 4)
     keep(2)
+    a2f(1)
     a3n(0)
-    a1(1)
+    axn(1)
     a3f(0)
-    a2r(1)
-    a2f(1)
+    early4(2)
+    early3(2)
+    axf(1)
+    send(0, 4)
+    send(1, 3)
+    send(2, 2)
     for l in range(LV):
         count(l)
     lax.fori_loop(0, NP, partners, 0)
     a4(0)
+    a2f(2)
     a3n(1)
     a3f(1)
-    a1(2)
-    a2r(2)
-    a2f(2)
+    axn(2)
+    axf(2)
+    send(1, 4)
+    send(2, 3, 4)
     a5(0)
     a4(1)
     a3n(2)
@@ -539,21 +581,42 @@
     a8(2)
     a9(2)
     forward(1)
-    settle(2)
-
-    def block(j):
-        cols = pl.ds(pl.multiple_of(j * PART, PART), PART)
-        return contract(h2[...], WR[2][:, :, cols].reshape(HID, PART), 1, 0) * scale_f
+    settle(2, 1)
+
+    def columns(j):
+        return pl.ds(pl.multiple_of(j * PART, PART), PART)
+
+    def mate_col(dy):
+        return lax.rem(y + dy, NY) * 2 + 1 - core
+
+    def most(j):
+        rows = [
+            WR[2][pl.ds(dx * NZ + 1, NZ - 1), :, columns(j)].reshape((NZ - 1) * B, PART)
+            for dx in range(NX)
+        ]
+        return contract(h2[...], jnp.concatenate(rows, axis=0), 1, 0)
+
+    def rest_of(j):
+        rows = [WR[2][dx * NZ, :, columns(j)] for dx in range(NX)]
+        return contract(h2b[...], jnp.concatenate(rows, axis=0), 1, 0)
+
+    def partials(dy, carry):
+        N1[dy] = most(mate_col(dy))
+        N0[dy] = most(ycol(dy))
+        return carry
+
+    lax.fori_loop(0, NY, partials, 0)
+    settle(2, 0, 1)
 
     def tsend(n, src, dst, other):
         remote(("t", n), zc, src, dst, ts.at[n], tr.at[n], "mp", other)
 
     def give(dy):
-        NS[dy] = block(lax.rem(y + dy, NY) * 2 + 1 - core).astype(bf16)
+        NS[dy] = ((N1[dy] + rest_of(mate_col(dy))) * scale_f).astype(bf16)
         tsend(dy, NS.at[dy], NR.at[dy], mate)
 
     def hold(dy):
-        N0[dy] = block(ycol(dy))
+        N0[dy] = (N0[dy] + rest_of(ycol(dy))) * scale_f
 
     sides = ((0, 1, *halves), (1, 3, *halves[::-1]))
     for dy in (2, 1, 3):
@@ -584,7 +647,8 @@
     out[...] = (
         N0[0] + NR[0].astype(f32) + TR[0].astype(f32) + TR[1].astype(f32)
     ).astype(bf16)
-    done = {id(xc[l, g, dx]) for l in range(LV) for g in range(5) for dx in range(1, NX)}
+    done = {id(xc[l, g, dx]) for l in range(LV) for g in range(2, 5) for dx in range(1, NX)}
+    done |= {id(zc[l, s, n]) for l in range(LV) for s in (0, 1) for n in range(10, 18)}
     for c in started:
         if id(c) not in done:
             c.wait_send()
@@ -598,8 +662,8 @@
     dense, dense_half = bf(M, B, D), bf(M, B, HALF)
     four, four_half = bf(NX, B, D), bf(NX, B, HALF)
     pairs = lambda kind: [kind] * (2 * LV)
-    scratch = [bf(NZ, NX, B, D)] * LV
-    for kind in (four_half, four, four_half, dense, dense, dense):
+    scratch = [bf(NZ - 3, NX, B, D)] * LV
+    for kind in (four_half, four, four_half, four, four_half, dense, dense, dense):
         scratch += pairs(kind)
     for kind in (dense, dense, dense_half, four_half, four_half, four_half, four_half):
         scratch += pairs(kind)
@@ -607,13 +671,13 @@
     scratch += [fl(M, B, D)] * LV + [dense] * LV
     scratch += [bf(NMP, ROWS, PART)] * 2
     scratch += [fl(NP, B, ROWS)] * 3
-    scratch += [bf(NP, B, ROWS)] * 4 + [fl(NP, B, PART), bf(ROWS, HID)]
-    scratch += [fl(NY, ROWS, PART), bf(NY, ROWS, PART), bf(NY, ROWS, PART)]
+    scratch += [bf(NP, B, ROWS)] * 4 + [fl(NP, B, PART), bf(ROWS, HID - NX * B), bf(ROWS, NX * B)]
+    scratch += [fl(NY, ROWS, PART), fl(NY, ROWS, PART), bf(NY, ROWS, PART), bf(NY, ROWS, PART)]
     scratch += [bf(2, HROW, PART)] * 2 + [bf(2, ROWS, PART)] * 2
     scratch += [pltpu.SMEM((LV * NZ * NX * M,), f32), pltpu.SMEM((LV * M,), f32)]
     scratch += [pltpu.SMEM(((LV + 2) * NP,), jnp.int32)]
     dma = pltpu.SemaphoreType.DMA
-    scratch += [dma((2, LV, 5, 3)), dma((2, LV, 5, 3)), dma((LV, 2, 10)), dma((LV, 2, 10))]
+    scratch += [dma((3, LV, 5, 3)), dma((3, LV, 5, 3)), dma((LV, 2, 18)), dma((LV, 2, 18))]
     scratch += [dma((20,)), dma((2, 10)), dma((2, 10)), dma((10,)), dma((10,))]
     smem = pl.BlockSpec(memory_space=pltpu.SMEM)
     anyw = pl.BlockSpec(memory_space=pl.ANY)

time: 272 us -> 266 us (0.978)
  Pallas kernels: 271 us -> 265 us
    pallas_call x1, Pallas kernels: 268 us -> 263 us  [step(): pl.pallas_call(step_kernel, out_shape=(jax.ShapeDtypeStruct((ROWS, PART),...]
where the time goes in v6:
time: 266 us
  Pallas kernels  265 us (100%)
    pallas_call x1, Pallas kernels, step(): pl.pallas_call(step_kernel, out_shape=(jax.ShapeDtypeStruct((ROWS, PART),...  263 us

profile of v6, /device:TPU:1, one launch (start us, length us, event | category | flops | bytes accessed | tf_op | source)
XLA Modules:
  0.0 265.6 jit_solution(2974885026085869654)
XLA Ops:
  0.6 262.6 %shard_map.86 = (bf16[384,256]{1,0:T(8,128)(2,1)}, bf16[3,8,16,2048]{3,2,1,0:T(8,128)(2,1)}) custom-call(s32[3,32]{1,0:T(4,128)} %assign.1, s32[3,8,32]{2,1,0:T(8,128)} %owners.1, bf16[384,256]{1,0:T(8,128)(2,1)} %tokens.1, bf16[384,256]{1,0:T(8,128)(2,1)} %cotangent.1, bf16[3,32,16,2048]{3,2,1,0:T(8,128)(2,1)} %bitcast.6, f32[3,8,16,2048]{3,2,1,0:T(8,128)} %bitcast.7, ...), custom_call_target="tpu_custom_call" | custom-call | tf_op jit(solution)/shard_map/pallas_call | solution.py:684
  263.3 2.4 shard_map.87
